TPU v7x, 256 devices: a whole 4x4x8 slice. The times are simulated.
256 devices in a mesh: space: 8 (over z_lo, y), vec: 32 (over x, z_hi, core).
Axes of the slice: x: 4, y: 4, z: 8 (z_hi: 4, z_lo: 2; z = z_hi * 2 + z_lo), core: 2. Of those that a mesh axis runs over, the one named last changes fastest.
Arguments:
- vectors: float32 [2, 3, 128, 8, 4096], P(None, None, 'vec', 'space'), may hold values from -6 to 6
- gauge_links: float32 [3, 2, 3, 3, 8, 4096], P(None, None, None, None, 'space'), may hold values from -2.5 to 2.5
- momenta: int32 [2, 3], replicated, may hold values from 1 to 2
- displacements: int32 [2], replicated, may hold values from 0 to 5
Outputs:
- elementals: float32 [2, 4, 128, 128], P(None, None, 'vec', 'space')
All inputs are finite; a program needn't handle non-finite values.
Results may differ from a plain program's by a relative error of at most 0.0003.
Values sent between devices are 32-bit elements; how exact they have to be, the bound alone decides.
No kernel may reach another device: no remote copies, remote signals or barrier semaphores. Data moves between devices by JAX's collectives and lax.ppermute only.
A program may use at most 128 MiB of HBM per device.

v0:
```python
import math

import jax
import jax.numpy as jnp
from jax import lax
from jax.sharding import PartitionSpec as P

NY = 64
NZ = 64
NMOM = 2
NDISP = 2


def extended(block, sides, width):
    for axis, dim in sides:
        count = lax.axis_size(axis)
        forward = [(i, i + 1) for i in range(count - 1)]
        forward.append((count - 1, 0))
        backward = [(target, source) for source, target in forward]
        low = lax.ppermute(
            lax.slice_in_dim(block, block.shape[dim] - width, None, axis=dim), axis, forward
        )
        high = lax.ppermute(lax.slice_in_dim(block, 0, width, axis=dim), axis, backward)
        block = jnp.concatenate([low, block, high], axis=dim)
    return block


def shifted(block, axis, distance):
    devices = range(lax.axis_size(axis))
    route = [((i - distance) % len(devices), i) for i in devices]
    return lax.ppermute(block, axis, route)


def colour_term(gauge_one, colour_field, colour, dagger):
    if dagger:
        link_re = gauge_one[0][colour][:, None]
        link_im = -gauge_one[1][colour][:, None]
    else:
        link_re = gauge_one[0][:, colour][:, None]
        link_im = gauge_one[1][:, colour][:, None]
    vec_re = colour_field[0][colour][None]
    vec_im = colour_field[1][colour][None]
    return (link_re * vec_re - link_im * vec_im, link_re * vec_im + link_im * vec_re)


def link_times(gauge_one, colour_field, dagger):
    real_sum, imag_sum = colour_term(gauge_one, colour_field, 0, dagger)
    for colour in (1, 2):
        real_next, imag_next = colour_term(gauge_one, colour_field, colour, dagger)
        real_sum = real_sum + real_next
        imag_sum = imag_sum + imag_next
    return jnp.stack([real_sum, imag_sum])


def roll_depth(colour_field, offset, row_len):
    total_len = colour_field.shape[-1]
    position = lax.broadcasted_iota(jnp.int32, (total_len,), 0) % row_len
    if offset > 0:
        inner_roll = jnp.roll(colour_field, -1, -1)
        outer_roll = jnp.roll(colour_field, row_len - 1, -1)
        return jnp.where(position == row_len - 1, outer_roll, inner_roll)
    inner_roll = jnp.roll(colour_field, 1, -1)
    outer_roll = jnp.roll(colour_field, 1 - row_len, -1)
    return jnp.where(position == 0, outer_roll, inner_roll)


def plane_pair(colour_field):
    padded = extended(colour_field, (("space", 3),), 1)
    return (padded[:, :, :, 2:], padded[:, :, :, :-2])


def slab_neighbours(colour_field):
    return (
        plane_pair(colour_field),
        (jnp.roll(colour_field, -NZ, 4), jnp.roll(colour_field, NZ, 4)),
        (roll_depth(colour_field, 1, NZ), roll_depth(colour_field, -1, NZ)),
    )


def six_hops(gauge_sites, gauge_back, neighbours):
    forward = [
        link_times(gauge_sites[direction], neighbours[direction][0], False)
        for direction in range(3)
    ]
    backward = [
        link_times(gauge_back[direction], neighbours[direction][1], True) for direction in range(3)
    ]
    return forward + backward


def hopping_sum(hop_list):
    running = hop_list[0]
    for hop_index in range(1, 6):
        running = running + hop_list[hop_index]
    return running


def pair_sums(left_side, right_side):
    hig = lax.Precision.HIGHEST
    real_part = jnp.einsum(
        "cixs,cjxs->ij", left_side[0], right_side[0], precision=hig
    ) + jnp.einsum("cixs,cjxs->ij", left_side[1], right_side[1], precision=hig)
    imag_part = jnp.einsum(
        "cixs,cjxs->ij", left_side[0], right_side[1], precision=hig
    ) - jnp.einsum("cixs,cjxs->ij", left_side[1], right_side[0], precision=hig)
    return (real_part, imag_part)


def local(vectors, gauge_links, momenta, displacements):
    planes = vectors.shape[3]
    global_planes = planes * lax.axis_size("space")
    edge_plane = shifted(gauge_links[0], "space", 1)
    back_plane = jnp.concatenate([edge_plane, gauge_links[0][:, :, :, :-1, :]], 3)
    back_row = jnp.roll(gauge_links[1], NZ, 4)
    back_depth = roll_depth(gauge_links[2], -1, NZ)
    gauge_back = jnp.stack([back_plane, back_row, back_depth])
    first_step = hopping_sum(six_hops(gauge_links, gauge_back, slab_neighbours(vectors))) / -6.0
    filtered = (
        hopping_sum(six_hops(gauge_links, gauge_back, slab_neighbours(first_step))) / -3.0 - vectors
    )
    slab_hops = jnp.stack(six_hops(gauge_links, gauge_back, slab_neighbours(filtered)))
    chosen = [
        lax.dynamic_index_in_dim(slab_hops, displacements[op_index], 0, False)
        for op_index in range(NDISP)
    ]
    exchanged = lax.all_to_all(
        jnp.stack([filtered] + chosen), "vec", split_axis=5, concat_axis=3, tiled=True
    )
    block_field = exchanged[0]
    displaced = [exchanged[1 + op_index] for op_index in range(NDISP)]
    block_len = block_field.shape[4]
    plane_index = lax.axis_index("space") * planes + jnp.arange(planes, dtype=jnp.int32)
    flat_index = lax.axis_index("vec") * block_len + jnp.arange(block_len, dtype=jnp.int32)
    row_index = flat_index // NZ
    depth_index = flat_index % NZ
    real_rows = []
    imag_rows = []
    for op_index in range(NMOM):
        phase_plane = (momenta[op_index, 0] * plane_index % global_planes).astype(
            jnp.float32
        ) / global_planes
        phase_row = (momenta[op_index, 1] * row_index % NY).astype(jnp.float32) / NY
        phase_depth = (momenta[op_index, 2] * depth_index % NZ).astype(jnp.float32) / NZ
        angle_grid = (phase_plane[:, None] + phase_row[None, :] + phase_depth[None, :]) * (
            2.0 * math.pi
        )
        cosine = jnp.cos(angle_grid)
        sine_part = jnp.sin(angle_grid)
        phased = jnp.stack(
            [
                cosine * block_field[0] - sine_part * block_field[1],
                cosine * block_field[1] + sine_part * block_field[0],
            ]
        )
        real_part, imag_part = pair_sums(block_field, phased)
        real_rows.append(real_part)
        imag_rows.append(imag_part)
    for op_index in range(NDISP):
        real_part, imag_part = pair_sums(block_field, displaced[op_index])
        real_rows.append(real_part)
        imag_rows.append(imag_part)
    partial_sums = jnp.stack([jnp.stack(real_rows), jnp.stack(imag_rows)])
    share_sums = lax.psum_scatter(partial_sums, "vec", scatter_dimension=2, tiled=True)
    whole_sums = lax.psum_scatter(share_sums, "space", scatter_dimension=3, tiled=True)
    norm_scale = 1.0 / math.sqrt(3 * global_planes * NY * NZ)
    return whole_sums * norm_scale


def solution(mesh):
    placed = (
        P(None, None, "vec", "space", None),
        P(None, None, None, None, "space", None),
        P(),
        P(),
    )
    return jax.shard_map(
        local, mesh=mesh, in_specs=placed, out_specs=P(None, None, "vec", "space"), check_vma=False
    )
```

profile of v0, /device:TPU:32, one launch (start us, length us, event | category | flops | bytes accessed | tf_op | source)
XLA Modules:
  0.0 636.4 jit_solution(12803463155827763475)
XLA Ops:
  6.5 1.6 collective-permute-start.2
  8.1 2.6 collective-permute-start
  10.7 1.9 slice_bitcast_fusion.1
  12.6 2.1 fusion.117
  14.8 0.9 fusion.120
  15.7 0.9 fusion.123
  17.7 3.8 broadcast_select_fusion.2
  22.5 0.7 broadcast_select_fusion.6
  23.7 0.7 fusion.62
  24.6 0.9 fusion.52
  26.7 1.1 add_bitcast_fusion.15
  27.8 1.1 add_bitcast_fusion.19
  29.0 1.1 add_bitcast_fusion.21
  30.1 1.9 add_bitcast_fusion.13
  32.0 0.7 fusion.132
  35.9 0.8 copy.552
  36.7 0.8 copy.553
  37.6 0.8 copy.554
  38.4 0.8 copy.555
  39.3 0.8 copy.557
  41.4 1.1 fusion.126
  42.8 1.0 fusion.118
  44.1 1.0 fusion.124
  45.4 1.3 add_bitcast_fusion.17
  46.8 1.1 add_bitcast_fusion.23
  47.9 1.9 fusion.18
  49.8 0.8 fusion.19
  50.6 4.1 collective-permute-start.3
  54.7 0.9 fusion.107
  55.7 0.9 fusion.110
  56.5 0.9 fusion.113
  58.9 0.9 broadcast_select_fusion.4
  60.2 0.9 fusion.42
  61.4 0.9 broadcast_select_fusion.1
  62.6 1.1 add_bitcast_fusion.9
  63.8 1.1 add_bitcast_fusion.7
  64.9 1.1 add_bitcast_fusion.3
  66.0 1.1 add_bitcast_fusion.1
  67.5 2.5 collective-permute-done.4
  70.3 1.1 add_bitcast_fusion.11
  71.5 1.3 add_bitcast_fusion.5
  72.8 2.2 fusion.30
  75.6 0.9 fusion.98
  76.4 0.9 fusion.99
  77.5 0.9 fusion.102
  78.6 4.1 collective-permute-start.5
  82.7 0.9 broadcast_select_fusion
  84.0 0.9 fusion.32
  85.2 0.9 broadcast_select_fusion.3
  88.7 0.8 collective-permute-done.6
  91.9 33.3 %copy.147 = f32[3,2,3,4,1,4096]{3,2,4,1,0,5:T(4,128)} copy(f32[3,2,3,4,1,4096]{5,3,2,1,4,0:T(4,128)S(1)} %pad_maximum_fusion) | data formatting | bytes 2359296 | tf_op jit(solution)/shard_map/stack | solution.py:127
  125.2 40.0 %reshape.3120 = f32[32,1,9216]{2,1,0:T(1,128)} reshape(f32[4096,3,2,1,3,4]{5,4,3,2,1,0:T(4,128)} %bitcast.634) | data formatting | bytes 2359296
  165.2 10.5 %all-to-all-start = ((f32[32,1,9216]{2,1,0:T(1,128)}), f32[32,1,9216]{2,1,0:T(1,128)S(1)}, u32[]{:S(2)}, u32[]{:S(2)}) async-start(f32[32,1,9216]{2,1,0:T(1,128)} %reshape.3120), calls=%async_computation | async-start | bytes 2359296 | tf_op jit(solution)/shard_map/all_to_all | solution.py:126
  178.1 2.7 fusion.92
  180.8 26.2 %all-to-all-done = f32[32,1,9216]{2,1,0:T(1,128)S(1)} async-done(((f32[32,1,9216]{2,1,0:T(1,128)}), f32[32,1,9216]{2,1,0:T(1,128)S(1)}, u32[]{:S(2)}, u32[]{:S(2)}) %all-to-all-start) | async-done | bytes 1179680 | tf_op jit(solution)/shard_map/all_to_all | solution.py:126
  207.6 3.4 reduce
  211.0 50.4 %reshape.3121 = f32[4096,3,2,1,3,4]{5,4,3,2,1,0:T(4,128)} reshape(f32[32,9216]{1,0:T(8,128)S(1)} %reduce) | data formatting | bytes 2359296
  261.4 36.2 %copy.148 = f32[3,2,3,4,1,4096]{5,4,3,2,1,0:T(1,128)S(1)} copy(f32[3,2,3,4,1,4096]{3,2,4,1,0,5:T(4,128)} %bitcast.635) | data formatting | bytes 2359296 | tf_op jit(solution)/shard_map/all_to_all | solution.py:126
  305.5 0.8 pad_maximum_fusion.1
  307.7 279.0 %all-reduce.3.cloned.1.call-done = f32[2,4,128,128]{3,2,1,0:T(8,128)} async-done(((f32[2,4,128,128]{3,2,1,0:T(8,128)}), f32[2,4,128,128]{3,2,1,0:T(8,128)}) %all-reduce.3.cloned.1.call-update) | async-done | bytes 524304
  586.7 0.8 constant_dynamic-slice_fusion
  587.7 1.0 reshape.3117
  588.7 38.9 %reduce-scatter.5.cloned.1.call-done = f32[16,32]{1,0:T(8,128)} async-done(((f32[128,32]{1,0:T(8,128)}), f32[16,32]{1,0:T(8,128)}) %reduce-scatter.5.cloned.1.call-update) | async-done | bytes 2064
  627.6 0.8 reshape.3118
  (230 shorter events, 25.5 us)
Async XLA Ops:
  6.5 8.1 %copy-start = (f32[2,3,4,1,4096]{4,3,2,1,0:T(1,128)S(1)}, f32[2,3,4,1,4096]{4,3,2,1,0:T(1,128)}, u32[]{:S(2)}) copy-start(f32[2,3,4,1,4096]{4,3,2,1,0:T(1,128)} %param.4) | copy-start | bytes 1179652
  6.5 36.2 %collective-permute-start.2 = (f32[2,3,4,1,4096]{4,3,2,1,0:T(1,128)}, f32[2,3,4,1,4096]{4,3,2,1,0:T(1,128)}, u32[]{:S(2)}, u32[]{:S(2)}) collective-permute-start(f32[2,3,4,1,4096]{4,3,2,1,0:T(1,128)} %param.4), channel_id=1, source_target_pairs={{0,32},{32,64},{64,96},{96,128},{128,160},{160,192},{192,224},{224... | collective-permute-start | bytes 1179656 | tf_op jit(solution)/shard_map/ppermute | solution.py:20
  8.1 36.0 %collective-permute-start = (f32[2,3,4,1,4096]{4,3,2,1,0:T(1,128)}, f32[2,3,4,1,4096]{4,3,2,1,0:T(1,128)}, u32[]{:S(2)}, u32[]{:S(2)}) collective-permute-start(f32[2,3,4,1,4096]{4,3,2,1,0:T(1,128)} %param.4), channel_id=1, source_target_pairs={{32,0},{64,32},{96,64},{128,96},{160,128},{192,160},{224,192},{0,2... | collective-permute-start | bytes 1179656 | tf_op jit(solution)/shard_map/ppermute | solution.py:23
  12.6 4.2 copy-start.1
  12.6 28.8 %collective-permute-start.1 = (f32[2,3,3,1,4096]{4,3,2,1,0:T(1,128)}, f32[2,3,3,1,4096]{4,3,2,1,0:T(1,128)}, u32[]{:S(2)}, u32[]{:S(2)}) collective-permute-start(f32[2,3,3,1,4096]{4,3,2,1,0:T(1,128)} %get-tuple-element.24), channel_id=1, source_target_pairs={{224,0},{0,32},{32,64},{64,96},{96,128},{128,160},{160,192},{192,2... | collective-permute-start | bytes 884744 | tf_op jit(solution)/shard_map/ppermute | solution.py:31
  27.8 4.8 copy-start.5
  45.4 4.4 copy-start.2
  45.4 4.4 copy-start.3
  50.6 16.6 %collective-permute-start.3 = (f32[2,3,4,1,4096]{4,3,2,1,0:T(1,128)S(1)}, f32[2,3,4,1,4096]{4,3,2,1,0:T(1,128)S(1)}, u32[]{:S(2)}, u32[]{:S(2)}) collective-permute-start(f32[2,3,4,1,4096]{4,3,2,1,0:T(1,128)S(1)} %fusion.19), channel_id=1, source_target_pairs={{32,0},{64,32},{96,64},{128,96},{160,128},{192,160},{224,192},{0,2... | collective-permute-start | bytes 1179656 | tf_op jit(solution)/shard_map/ppermute | solution.py:23
  57.6 12.4 %collective-permute-start.4 = (f32[2,3,4,1,4096]{4,3,2,1,0:T(1,128)S(1)}, f32[2,3,4,1,4096]{4,3,2,1,0:T(1,128)S(1)}, u32[]{:S(2)}, u32[]{:S(2)}) collective-permute-start(f32[2,3,4,1,4096]{4,3,2,1,0:T(1,128)S(1)} %fusion.19), channel_id=1, source_target_pairs={{0,32},{32,64},{64,96},{96,128},{128,160},{160,192},{192,224},{224... | collective-permute-start | bytes 1179656 | tf_op jit(solution)/shard_map/ppermute | solution.py:20
  78.5 11.0 %collective-permute-start.6 = (f32[2,3,4,1,4096]{4,3,2,1,0:T(1,128)S(1)}, f32[2,3,4,1,4096]{4,3,2,1,0:T(1,128)S(1)}, u32[]{:S(2)}, u32[]{:S(2)}) collective-permute-start(f32[2,3,4,1,4096]{4,3,2,1,0:T(1,128)S(1)} %copy_subtract_fusion), channel_id=1, source_target_pairs={{0,32},{32,64},{64,96},{96,128},{128,160},{160,192},{192,224},{224... | collective-permute-start | bytes 1179656 | tf_op jit(solution)/shard_map/ppermute | solution.py:20
  78.6 11.3 %collective-permute-start.5 = (f32[2,3,4,1,4096]{4,3,2,1,0:T(1,128)S(1)}, f32[2,3,4,1,4096]{4,3,2,1,0:T(1,128)S(1)}, u32[]{:S(2)}, u32[]{:S(2)}) collective-permute-start(f32[2,3,4,1,4096]{4,3,2,1,0:T(1,128)S(1)} %copy_subtract_fusion), channel_id=1, source_target_pairs={{32,0},{64,32},{96,64},{128,96},{160,128},{192,160},{224,192},{0,2... | collective-permute-start | bytes 1179656 | tf_op jit(solution)/shard_map/ppermute | solution.py:23
  165.2 10.8 %copy-start.4 = (s32[2,3]{1,0:T(2,128)S(1)}, s32[2,3]{1,0:T(2,128)}, u32[]{:S(2)}) copy-start(s32[2,3]{1,0:T(2,128)} %param.6) | copy-start | bytes 76
  165.2 41.8 %all-to-all-start = ((f32[32,1,9216]{2,1,0:T(1,128)}), f32[32,1,9216]{2,1,0:T(1,128)S(1)}, u32[]{:S(2)}, u32[]{:S(2)}) async-start(f32[32,1,9216]{2,1,0:T(1,128)} %reshape.3120), calls=%async_computation | async-start | bytes 2359296 | tf_op jit(solution)/shard_map/all_to_all | solution.py:126
  175.8 410.9 %all-reduce.3.cloned.1.call-start = ((), (), s32[]{:S(2)}) async-start(), calls=%async_computation.3 | async-start | bytes 1048576
  303.9 2.5 copy-start.6
  306.4 321.2 %reduce-scatter.5.cloned.1.call-start = ((), (), s32[]{:S(2)}) async-start(), calls=%async_computation.2 | async-start | bytes 73728
Sparse Core Ops, SparseCore 0:
  306.5 280.1 all-reduce.2
  589.3 38.2 reduce-scatter.4
where the time goes:
time: 646 us; the launch traced here: 636 us
  waiting for transfers between devices  347 us (54%)
  local copies, waits for them, and re-layouts  193 us (30%)
  other arithmetic  44.6 us (7%)
  starting transfers between devices  23.9 us (4%)
  between operations  21.3 us (3%)
    unnamed x4, waiting for transfers between devices  318 us
    unnamed x146, local copies, waits for them, and re-layouts  104 us
    all_to_all x2, local copies, waits for them, and re-layouts, local(): lax.all_to_all(jnp.stack([filtered] + chosen), 'vec', split_axis=5, conca...  36.7 us
    another operation x1, local copies, waits for them, and re-layouts, local(): jnp.stack([filtered] + chosen)  33.3 us
    all_to_all x1, waiting for transfers between devices, local(): lax.all_to_all(jnp.stack([filtered] + chosen), 'vec', split_axis=5, conca...  26.2 us
    another operation x12, other arithmetic, link_times(): return jnp.stack([real_sum, imag_sum])  14.6 us
  transfers between devices with their start and end apart: 10, of which 5 were waited for; matrix products, arithmetic and copies ran while one was open for 8% of the time, Pallas kernels for 0%

commit v1 on v0

v1 whole, which is shorter than its diff:
```python
import functools
import math

import jax
import jax.numpy as jnp
from jax import lax
from jax.experimental import pallas as pl
from jax.experimental.pallas import tpu as pltpu
from jax.sharding import PartitionSpec as P

NY = 64
NZ = 64
NMOM = 2
NDISP = 2
ROWS = 32
LANES = 128
VMEM = pltpu.VMEM
F32 = jnp.float32


def call(body, out_shape, n_in, scratch=(), scalars=False, flops=0, nbytes=0):
    specs = [pl.BlockSpec(memory_space=VMEM)] * n_in
    if scalars:
        specs = [pl.BlockSpec(memory_space=pltpu.SMEM)] + specs
    many = isinstance(out_shape, (list, tuple))
    return pl.pallas_call(
        body,
        out_shape=out_shape,
        in_specs=specs,
        out_specs=[pl.BlockSpec(memory_space=VMEM)] * len(out_shape)
        if many
        else pl.BlockSpec(memory_space=VMEM),
        scratch_shapes=list(scratch),
        cost_estimate=pl.CostEstimate(flops=flops, bytes_accessed=nbytes, transcendentals=0),
    )


def struct(*shape):
    return jax.ShapeDtypeStruct(shape, F32)


def times(link, field):
    out = []
    for i in range(3):
        re = im = None
        for j in range(3):
            a, b = link(0, i, j), link(1, i, j)
            x, y = field[j], field[3 + j]
            re_j, im_j = a * x - b * y, a * y + b * x
            re = re_j if re is None else re + re_j
            im = im_j if im is None else im + im_j
        out.append((re, im))
    return [o[0] for o in out] + [o[1] for o in out]


def times_dagger(link, field):
    out = []
    for i in range(3):
        re = im = None
        for j in range(3):
            a, b = link(0, j, i), link(1, j, i)
            x, y = field[j], field[3 + j]
            re_j, im_j = a * x + b * y, a * y - b * x
            re = re_j if re is None else re + re_j
            im = im_j if im is None else im + im_j
        out.append((re, im))
    return [o[0] for o in out] + [o[1] for o in out]


def lane_of(shape):
    return lax.broadcasted_iota(jnp.int32, shape, len(shape) - 1)


def z_next(x):
    axis = x.ndim - 1
    end = lane_of(x.shape) % NZ == NZ - 1
    return jnp.where(end, pltpu.roll(x, NZ - 1, axis), pltpu.roll(x, LANES - 1, axis))


def z_prev(x):
    axis = x.ndim - 1
    start = lane_of(x.shape) % NZ == 0
    return jnp.where(start, pltpu.roll(x, LANES - NZ + 1, axis), pltpu.roll(x, 1, axis))


def y_next(x):
    half = pltpu.roll(x, NZ, 1)
    return jnp.where(lane_of(x.shape) < NZ, half, pltpu.roll(half, ROWS - 1, 0))


def y_prev(x):
    half = pltpu.roll(x, NZ, 1)
    return jnp.where(lane_of(x.shape) < NZ, pltpu.roll(half, 1, 0), half)


def plane_link(g_ref, direction):
    return lambda reim, row, col: g_ref[direction * 18 + reim * 9 + row * 3 + col]


def start_body(sc, v_ref, g_ref, w_ref):
    link = plane_link(g_ref, 0)

    def one(n, carry):
        out = times_dagger(link, [v_ref[4 * k + n] for k in range(6)])
        for k in range(6):
            w_ref[pl.ds((4 * k + n) * ROWS, ROWS), :] = out[k]
        return carry

    lax.fori_loop(0, 4, one, 0)
    block = sc[0]
    for n in range(18):
        w_ref[24 * ROWS + 2 * n : 24 * ROWS + 2 * n + 2, :] = g_ref[n, pl.ds(2 * block, 2), :]
    w_ref[24 * ROWS + 36 :, :] = jnp.zeros((4, LANES), F32)


def inner_body(v_ref, g_ref, acc_ref):
    link_y, link_z = plane_link(g_ref, 1), plane_link(g_ref, 2)

    def one(n, carry):
        field = [v_ref[4 * k + n] for k in range(6)]
        total = times(link_y, [y_next(x) for x in field])
        for part in (
            [y_prev(x) for x in times_dagger(link_y, field)],
            times(link_z, [z_next(x) for x in field]),
            [z_prev(x) for x in times_dagger(link_z, field)],
        ):
            total = [a + b for a, b in zip(total, part)]
        for k in range(6):
            acc_ref[4 * k + n] = total[k]
        return carry

    lax.fori_loop(0, 4, one, 0)


def first_body(acc_ref, ahead_ref, behind_ref, g_ref, first_ref, w_ref):
    link = plane_link(g_ref, 0)

    def one(n, carry):
        hop = times(link, [ahead_ref[4 * k + n] for k in range(6)])
        first = [
            (acc_ref[4 * k + n] + hop[k] + behind_ref[pl.ds((4 * k + n) * ROWS, ROWS), :]) / -6.0
            for k in range(6)
        ]
        out = times_dagger(link, first)
        for k in range(6):
            first_ref[4 * k + n] = first[k]
            w_ref[4 * k + n] = out[k]
        return carry

    lax.fori_loop(0, 4, one, 0)


def second_body(acc_ref, ahead_ref, behind_ref, v_ref, g_ref, out_ref, f_ref, half_ref):
    link = plane_link(g_ref, 0)

    def one(n, carry):
        hop = times(link, [ahead_ref[4 * k + n] for k in range(6)])
        for k in range(6):
            r = 4 * k + n
            f = (acc_ref[r] + hop[k] + behind_ref[r]) / -3.0 - v_ref[r]
            f_ref[pl.ds(r * ROWS, ROWS), :] = f
            half_ref[pl.ds(r * ROWS, ROWS), :] = pltpu.roll(f, NZ, 1)
        return carry

    lax.fori_loop(0, 4, one, 0)
    low = lane_of((24, LANES)) < NZ
    for block in range(16):
        for q in range(2):
            out_ref[block, 24 * q : 24 * q + 24, :] = f_ref[pl.ds(2 * block + q, 24, ROWS), :]
        under = half_ref[pl.ds((2 * block - 1) % ROWS, 24, ROWS), :]
        over = half_ref[pl.ds((2 * block + 2) % ROWS, 24, ROWS), :]
        out_ref[block, 48:72, :] = jnp.where(low, under, over)


def matrix_body(sc, g_ref, behind_ref, m_ref):
    block = sc[0]
    low = lane_of((1, LANES)) < NZ
    for op in range(NDISP):
        hop = lax.rem(sc[2 + op] + 3, 6)
        direction = lax.rem(hop, 3)

        def put(reim, row, col, q, value):
            m_ref[pl.ds(((op * 18 + reim * 9 + row * 3 + col) * 2) + q, 1), :] = value

        @pl.when(hop < 3)
        def _():
            for n in range(18):
                for q in range(2):
                    m_ref[pl.ds((op * 18 + n) * 2 + q, 1), :] = g_ref[
                        direction * 18 + n, pl.ds(2 * block + q, 1), :
                    ]

        def dagger(rows_of):
            for reim in range(2):
                for row in range(3):
                    for col in range(3):
                        n = reim * 9 + col * 3 + row
                        for q in range(2):
                            value = rows_of(n, q)
                            put(reim, row, col, q, -value if reim else value)

        @pl.when(hop == 3)
        def _():
            dagger(lambda n, q: behind_ref[24 * ROWS + 2 * n + q : 24 * ROWS + 2 * n + q + 1, :])

        @pl.when(hop == 4)
        def _():
            def rows_of(n, q):
                under = g_ref[18 + n, pl.ds(lax.rem(2 * block + q + ROWS - 1, ROWS), 1), :]
                here = g_ref[18 + n, pl.ds(2 * block + q, 1), :]
                return pltpu.roll(jnp.where(low, here, under), NZ, 1)

            dagger(rows_of)

        @pl.when(hop == 5)
        def _():
            dagger(lambda n, q: z_prev(g_ref[36 + n, pl.ds(2 * block + q, 1), :]))


def rows_of_block(ref, tile, odd):
    both = ref[:, 8 * tile : 8 * tile + 8, :].reshape(8, 2, 8, LANES)
    left, right = both[:, 0], both[:, 1]
    low = lax.broadcasted_iota(jnp.int32, left.shape, 1) < 4
    if odd:
        mixed = jnp.where(low, pltpu.roll(left, 4, 1), right)
    else:
        mixed = jnp.where(low, left, pltpu.roll(right, 4, 1))
    return mixed.reshape(64, LANES)


def split(x):
    high = x.astype(jnp.bfloat16)
    return high, (x - high.astype(F32)).astype(jnp.bfloat16)


def gram_body(
    scale, sc, own_ref, other_ref, ahead_ref, behind_ref, m_ref, ph_ref, out_ref,
    f_ref, n_ref, lhs_hi, lhs_lo, rhs_hi, rhs_lo,
):
    core = sc[1]

    def column(k, q):
        return slice((2 * k + q) * LANES, (2 * k + q + 1) * LANES)

    def put_lhs(op, k, q, value):
        high, rest = split(value)
        lhs_hi[64 * op : 64 * op + 64, column(k, q)] = high
        lhs_lo[64 * op : 64 * op + 64, column(k, q)] = rest

    for q in range(2):
        for pair in range(3):
            tile = 3 * q + pair
            own = own_ref[:, 8 * tile : 8 * tile + 8, :]
            other = other_ref[:, 8 * tile : 8 * tile + 8, :]
            zero = jnp.where(core == 0, own, other)
            one = jnp.where(core == 0, other, own)
            low = lax.broadcasted_iota(jnp.int32, own.shape, 1) < 4
            even = jnp.where(low, zero, pltpu.roll(one, 4, 1)).reshape(128, LANES)
            odd = jnp.where(low, pltpu.roll(zero, 4, 1), one).reshape(128, LANES)
            for k, value in ((2 * pair, even), (2 * pair + 1, odd)):
                high, rest = split(value)
                for part, ref in ((high, rhs_hi), (rest, rhs_lo)):
                    ref[0:128, column(k, q)] = part
                    if k < 3:
                        ref[128:256, column(k + 3, q)] = -part
                    else:
                        ref[128:256, column(k - 3, q)] = part
            for odd_one in (0, 1):
                f_ref[2 * pair + odd_one, q] = rows_of_block(own_ref, tile, odd_one)
    for q in range(2):
        for op in range(NMOM):
            cosine = ph_ref[4 * op + q : 4 * op + q + 1, :]
            sine = ph_ref[4 * op + 2 + q : 4 * op + 3 + q, :]
            for c in range(3):
                re, im = f_ref[c, q], f_ref[3 + c, q]
                put_lhs(op, c, q, cosine * re + sine * im)
                put_lhs(op, 3 + c, q, cosine * im - sine * re)
    low = lane_of((64, LANES)) < NZ
    for op in range(NDISP):
        hop = lax.rem(sc[2 + op] + 3, 6)

        for which, ref in ((0, ahead_ref), (3, behind_ref)):

            @pl.when(hop == which)
            def _():
                for k in range(6):
                    for q in range(2):
                        n_ref[k, q] = rows_of_block(ref, 3 * q + k // 2, k % 2)

        @pl.when(hop == 1)
        def _():
            for k in range(6):
                edge = rows_of_block(own_ref, 6 + k // 2, k % 2)
                here, over = pltpu.roll(f_ref[k, 0], NZ, 1), pltpu.roll(f_ref[k, 1], NZ, 1)
                n_ref[k, 0] = jnp.where(low, here, over)
                n_ref[k, 1] = jnp.where(low, over, edge)

        @pl.when(hop == 4)
        def _():
            for k in range(6):
                edge = rows_of_block(own_ref, 6 + k // 2, k % 2)
                here, over = pltpu.roll(f_ref[k, 0], NZ, 1), pltpu.roll(f_ref[k, 1], NZ, 1)
                n_ref[k, 0] = jnp.where(low, edge, here)
                n_ref[k, 1] = jnp.where(low, here, over)

        @pl.when(hop == 2)
        def _():
            for k in range(6):
                for q in range(2):
                    n_ref[k, q] = z_next(f_ref[k, q])

        @pl.when(hop == 5)
        def _():
            for k in range(6):
                for q in range(2):
                    n_ref[k, q] = z_prev(f_ref[k, q])

        for q in range(2):

            def link(reim, row, col):
                at = (op * 18 + reim * 9 + row * 3 + col) * 2 + q
                return m_ref[at : at + 1, :]

            moved = times(link, [n_ref[k, q] for k in range(6)])
            for k in range(6):
                put_lhs(NMOM + op, k, q, moved[k])

    def dot(a, b):
        return lax.dot_general(
            a[...], b[...], (((1,), (1,)), ((), ())), preferred_element_type=F32
        )

    sums = dot(lhs_hi, rhs_hi) + (dot(lhs_hi, rhs_lo) + dot(lhs_lo, rhs_hi))
    tiles = [
        sums[64 * op : 64 * op + 64, 128 * reim : 128 * reim + 128] * scale
        for reim in range(2)
        for op in range(4)
    ]
    group = lane_of((64, LANES)) // 16
    for bit in (4, 2, 1):
        clear = lax.rem(group // bit, 2) == 0
        for i in range(8):
            if i & bit == 0:
                a, b = tiles[i], tiles[i + bit]
                tiles[i] = jnp.where(clear, a, pltpu.roll(b, 16 * bit, 1))
                tiles[i + bit] = jnp.where(clear, pltpu.roll(a, LANES - 16 * bit, 1), b)
    for slab in range(8):
        out_ref[slab] = tiles[slab]


def finish_body(part_ref, out_ref):
    parts = [part_ref[8 * i : 8 * i + 8, :] for i in range(64)]
    while len(parts) > 1:
        parts = [a + b for a, b in zip(parts[::2], parts[1::2])]
    total = parts[0] + pltpu.roll(parts[0], 4, 0)
    for t in range(8):
        moved = total if t == 0 else pltpu.roll(total, LANES - 16 * t, 1)
        out_ref[t] = moved[:4, :16]


def local(slabs, vecs, vectors, gauge_links, momenta, displacements):
    field_bytes = 24 * ROWS * LANES * 4
    field = vectors.reshape(24, ROWS, LANES)
    gauge = gauge_links.reshape(54, ROWS, LANES)
    slab = lax.axis_index("space")
    block = lax.axis_index("vec") // 2
    core = lax.axis_index("vec") % 2
    scalars = jnp.concatenate(
        [jnp.stack([block, core]).astype(jnp.int32), displacements.astype(jnp.int32)]
    )
    up = [(i, (i + 1) % slabs) for i in range(slabs)]
    down = [(i, (i - 1) % slabs) for i in range(slabs)]
    partner = [(i, i ^ 1) for i in range(vecs)]
    cores = [[2 * i + c for i in range(vecs // 2)] for c in range(2)]
    alike = [[2 * i + c for i in range(slabs * vecs // 2)] for c in range(2)]

    ahead = lax.ppermute(field, "space", down)
    shape = struct(24 * ROWS + 40, LANES)
    gauge_x = gauge[:18]
    w = call(start_body, shape, 2, scalars=True, flops=3 << 20, nbytes=3 * field_bytes)(
        scalars, field, gauge_x
    )
    behind = lax.ppermute(w, "space", up)
    inner = call(
        inner_body, struct(24, ROWS, LANES), 2, flops=12 << 20, nbytes=5 * field_bytes
    )
    acc = inner(field, gauge)
    first, w = call(
        first_body, [struct(24, ROWS, LANES)] * 2, 4, flops=6 << 20, nbytes=6 * field_bytes
    )(acc, ahead, behind, gauge_x)
    ahead2 = lax.ppermute(first, "space", down)
    behind2 = lax.ppermute(w, "space", up)
    acc = inner(first, gauge)
    matrices = call(
        matrix_body, struct(72, LANES), 2, scalars=True, flops=1 << 20, nbytes=4 * field_bytes
    )(scalars, gauge, behind)
    lane = jnp.arange(LANES, dtype=jnp.int32)
    row = 4 * block + 2 * jnp.arange(2, dtype=jnp.int32)[:, None] + lane[None, :] // NZ
    depth = jnp.broadcast_to(lane % NZ, row.shape)
    angles = []
    for op in range(NMOM):
        part_x = (momenta[op, 0] * slab % slabs).astype(F32) / slabs
        part_y = (momenta[op, 1] * row % NY).astype(F32) / NY
        part_z = (momenta[op, 2] * depth % NZ).astype(F32) / NZ
        angles.append((part_x + part_y + part_z) * (2.0 * math.pi))
    angle = jnp.stack(angles)
    phases = jnp.stack([jnp.cos(angle), jnp.sin(angle)], axis=1).reshape(8, LANES)
    cut = call(
        second_body,
        struct(16, 72, LANES),
        5,
        scratch=[VMEM((24 * ROWS, LANES), F32)] * 2,
        flops=6 << 20,
        nbytes=7 * field_bytes,
    )(acc, ahead2, behind2, field, gauge_x)
    own = lax.all_to_all(cut, "vec", 0, 0, axis_index_groups=cores)
    bulk = own[:, :48]
    ahead3 = lax.ppermute(bulk, "space", down)
    behind3 = lax.ppermute(bulk, "space", up)
    other = lax.ppermute(bulk, "vec", partner)
    scale = 1.0 / math.sqrt(3 * slabs * NY * NZ)
    sums = call(
        functools.partial(gram_body, scale),
        struct(slabs, 64, LANES),
        6,
        scratch=[VMEM((6, 2, 64, LANES), F32)] * 2
        + [VMEM((256, 12 * LANES), jnp.bfloat16)] * 4,
        scalars=True,
        flops=600 << 20,
        nbytes=6 * field_bytes,
    )(scalars, own, other, ahead3, behind3, matrices, phases)
    sums = sums.reshape(slabs * vecs // 2, 4, LANES)
    parts = lax.all_to_all(sums, ("space", "vec"), 0, 0, axis_index_groups=alike)
    out = call(finish_body, struct(8, 4, 16), 1)(parts.reshape(512, LANES))
    return out.reshape(2, 4, 4, 16)


def solution(mesh):
    placed = (
        P(None, None, "vec", "space", None),
        P(None, None, None, None, "space", None),
        P(),
        P(),
    )
    body = functools.partial(local, mesh.shape["space"], mesh.shape["vec"])
    return jax.shard_map(
        body, mesh=mesh, in_specs=placed, out_specs=P(None, None, "vec", "space"), check_vma=False
    )
```

time: 646 us -> 108 us (0.17); the launches traced: 636 us -> 108 us
  waiting for transfers between devices: 347 us -> 26.7 us
  local copies, waits for them, and re-layouts: 193 us -> 7.02 us
  other arithmetic: 44.6 us -> 5.11 us
  blocking collectives: 0 us -> 22.7 us
  Pallas kernels: 0 us -> 22 us
  between operations: 21.3 us -> 1.42 us
    unnamed x4 -> x0, waiting for transfers between devices: 318 us -> none
    unnamed x146 -> x22, local copies, waits for them, and re-layouts: 104 us -> 4.65 us
    all_to_all x2 -> x0, local copies, waits for them, and re-layouts: 36.7 us -> none  [local(): lax.all_to_all(jnp.stack([filtered] + chosen), 'vec', split_axis=5, conca...]
    another operation x1 -> x0, local copies, waits for them, and re-layouts: 33.3 us -> none  [local(): jnp.stack([filtered] + chosen)]
    all_to_all x0 -> x1, blocking collectives: none -> 22.7 us  [local(): lax.all_to_all(sums, ('space', 'vec'), 0, 0, axis_index_groups=alike)]
    pallas_call x0 -> x8, Pallas kernels: none -> 22 us  [the longest x1 4.25 us: local(): call(functools.partial(gram_body, scale), struct(slabs, 64, LANES), 6, sc...]
    another operation x17 -> x2, other arithmetic: 15.9 us -> 1.93 us  [the longest x1 1.33 us: local(): angle = jnp.stack(angles)]
    slice x45 -> x3, local copies, waits for them, and re-layouts: 16 us -> 2.38 us  [the longest x1 1.7 us: local(): gauge_x = gauge[:18]]
  transfers between devices with their start and end apart: 10 -> 8, of which waited for: 5 -> 5; matrix products, arithmetic and copies ran while one was open for 8% -> 5% of each run, Pallas kernels for 0% -> 8%
where the time goes in v1:
time: 108 us
  waiting for transfers between devices  26.7 us (25%)
  blocking collectives  22.7 us (21%)
  starting transfers between devices  22.6 us (21%)
  Pallas kernels  22 us (20%)
  local copies, waits for them, and re-layouts  7.02 us (6%)
  other arithmetic  5.11 us (5%)
  between operations  1.42 us (1%)
    all_to_all x1, blocking collectives, local(): lax.all_to_all(sums, ('space', 'vec'), 0, 0, axis_index_groups=alike)  22.7 us
    all_to_all x1, waiting for transfers between devices, local(): own = lax.all_to_all(cut, 'vec', 0, 0, axis_index_groups=cores)  12.8 us
    all_to_all x1, starting transfers between devices, local(): own = lax.all_to_all(cut, 'vec', 0, 0, axis_index_groups=cores)  10.1 us
    ppermute x1, waiting for transfers between devices, local(): behind2 = lax.ppermute(w, 'space', up)  5.11 us
    ppermute x1, waiting for transfers between devices, local(): ahead = lax.ppermute(field, 'space', down)  5.03 us
    unnamed x22, local copies, waits for them, and re-layouts  4.65 us
    pallas_call x1, Pallas kernels, local(): call(functools.partial(gram_body, scale), struct(slabs, 64, LANES), 6, sc...  4.25 us
    ppermute x1, starting transfers between devices, local(): ahead3 = lax.ppermute(bulk, 'space', down)  4.12 us
  transfers between devices with their start and end apart: 8, of which 5 were waited for; matrix products, arithmetic and copies ran while one was open for 5% of the time, Pallas kernels for 8%

profile of v1, /device:TPU:32, one launch (start us, length us, event | category | flops | bytes accessed | tf_op | source)
XLA Modules:
  0.0 107.6 jit_solution(14684749212162813611)
XLA Ops:
  0.0 1.7 %slice.27 = f32[1,2,3,3,1,4096]{5,4,3,2,1,0:T(1,128)} slice(f32[3,2,3,3,1,4096]{5,4,3,2,1,0:T(1,128)} %param.5), slice={[0:1], [0:2], [0:3], [0:3], [0:1], [0:4096]} | slice | bytes 589824 | tf_op jit(solution)/shard_map/slice | solution.py:379
  1.7 0.0 copy-start.7
  1.7 0.7 copy-done.7
  2.4 0.6 pad_add_fusion.sc
  3.0 0.0 copy-start
  3.0 2.1 %shard_map.47 = f32[808,128]{1,0:T(8,128)} custom-call(s32[4]{0:T(128)} %pad_add_fusion.sc, f32[24,32,128]{2,1,0:T(8,128)} %bitcast.25, f32[18,32,128]{2,1,0:T(8,128)} %bitcast.22), custom_call_target="tpu_custom_call" | custom-call | flops 3145728 | bytes 1179648 | tf_op jit(solution)/shard_map/pallas_call | solution.py:380
  5.0 1.6 %collective-permute-start.1 = (f32[808,128]{1,0:T(8,128)}, f32[808,128]{1,0:T(8,128)S(1)}, u32[]{:S(2)}, u32[]{:S(2)}) collective-permute-start(f32[808,128]{1,0:T(8,128)} %shard_map.47), channel_id=1, source_target_pairs={{0,32},{32,64},{64,96},{96,128},{128,160},{160,192},{192,224},{224... | collective-permute-start | bytes 1241096 | tf_op jit(solution)/shard_map/ppermute | solution.py:383
  6.6 0.0 copy-done
  6.6 2.6 %collective-permute-start = (f32[24,32,128]{2,1,0:T(8,128)S(1)}, f32[24,32,128]{2,1,0:T(8,128)S(1)}, u32[]{:S(2)}, u32[]{:S(2)}) collective-permute-start(f32[24,32,128]{2,1,0:T(8,128)S(1)} %bitcast.28), channel_id=1, source_target_pairs={{0,224},{32,0},{64,32},{96,64},{128,96},{160,128},{192,160},{224,1... | collective-permute-start | bytes 1179656 | tf_op jit(solution)/shard_map/ppermute | solution.py:377
  9.2 3.1 %shard_map.46.acc_ref = f32[24,32,128]{2,1,0:T(8,128)} custom-call(f32[24,32,128]{2,1,0:T(8,128)} %bitcast.26, f32[54,32,128]{2,1,0:T(8,128)} %bitcast.19), custom_call_target="tpu_custom_call" | custom-call | flops 12582912 | bytes 1966080 | tf_op jit(solution)/shard_map/pallas_call | solution.py:387
  12.3 5.0 %collective-permute-done.ahead_ref = f32[24,32,128]{2,1,0:T(8,128)S(1)} collective-permute-done((f32[24,32,128]{2,1,0:T(8,128)S(1)}, f32[24,32,128]{2,1,0:T(8,128)S(1)}, u32[]{:S(2)}, u32[]{:S(2)}) %collective-permute-start) | collective-permute-done | bytes 393248 | tf_op jit(solution)/shard_map/ppermute | solution.py:377
  17.3 0.0 copy-start.5
  17.3 1.4 %collective-permute-done.1.behind_ref = f32[808,128]{1,0:T(8,128)S(1)} collective-permute-done((f32[808,128]{1,0:T(8,128)}, f32[808,128]{1,0:T(8,128)S(1)}, u32[]{:S(2)}, u32[]{:S(2)}) %collective-permute-start.1) | collective-permute-done | bytes 413728 | tf_op jit(solution)/shard_map/ppermute | solution.py:383
  18.7 0.0 copy-done.5
  18.7 0.0 copy-start.1
  18.7 0.8 copy-done.1
  19.4 2.6 %shard_map.48 = (f32[24,32,128]{2,1,0:T(8,128)}, f32[24,32,128]{2,1,0:T(8,128)}) custom-call(f32[24,32,128]{2,1,0:T(8,128)} %shard_map.46.acc_ref, f32[24,32,128]{2,1,0:T(8,128)} %copy-done.5, f32[808,128]{1,0:T(8,128)} %copy-done.1, f32[18,32,128]{2,1,0:T(8,128)} %bitcast.23), custom_call_target="tpu_custom_call" | custom-call | flops 6291456 | bytes 2359296 | tf_op jit(solution)/shard_map/pallas_call | solution.py:388
  22.0 0.9 collective-permute-start.3
  22.9 3.3 %collective-permute-start.2 = (f32[24,32,128]{2,1,0:T(8,128)}, f32[24,32,128]{2,1,0:T(8,128)S(1)}, u32[]{:S(2)}, u32[]{:S(2)}) collective-permute-start(f32[24,32,128]{2,1,0:T(8,128)} %get-tuple-element.7.v_ref), channel_id=1, source_target_pairs={{0,224},{32,0},{64,32},{96,64},{128,96},{160,128},{192,160},{224,1... | collective-permute-start | bytes 1179656 | tf_op jit(solution)/shard_map/ppermute | solution.py:391
  26.1 3.1 %shard_map.49.acc_ref = f32[24,32,128]{2,1,0:T(8,128)} custom-call(f32[24,32,128]{2,1,0:T(8,128)} %get-tuple-element.7.v_ref, f32[54,32,128]{2,1,0:T(8,128)} %bitcast.20), custom_call_target="tpu_custom_call" | custom-call | flops 12582912 | bytes 1966080 | tf_op jit(solution)/shard_map/pallas_call | solution.py:393
  29.2 5.1 %collective-permute-done.3.behind_ref = f32[24,32,128]{2,1,0:T(8,128)S(1)} collective-permute-done((f32[24,32,128]{2,1,0:T(8,128)}, f32[24,32,128]{2,1,0:T(8,128)S(1)}, u32[]{:S(2)}, u32[]{:S(2)}) %collective-permute-start.3) | collective-permute-done | bytes 393248 | tf_op jit(solution)/shard_map/ppermute | solution.py:392
  34.3 0.0 copy-start.3
  34.3 0.0 collective-permute-done.2.ahead_ref
  34.3 0.7 copy-done.3
  35.1 0.0 copy-start.4
  35.1 0.8 copy-done.4
  35.8 3.2 %shard_map.50 = f32[16,72,128]{2,1,0:T(8,128)} custom-call(f32[24,32,128]{2,1,0:T(8,128)} %shard_map.49.acc_ref, f32[24,32,128]{2,1,0:T(8,128)} %copy-done.4, f32[24,32,128]{2,1,0:T(8,128)} %copy-done.3, f32[24,32,128]{2,1,0:T(8,128)} %bitcast.27, f32[18,32,128]{2,1,0:T(8,128)} %bitcast.24), custom_call_target="tpu_custom_call" | custom-call | flops 6291456 | bytes 2752512 | tf_op jit(solution)/shard_map/pallas_call | solution.py:408
  39.1 10.1 %all-to-all-start = ((f32[16,72,128]{2,1,0:T(8,128)}), f32[16,72,128]{2,1,0:T(8,128)S(1)}, u32[]{:S(2)}, u32[]{:S(2)}) async-start(f32[16,72,128]{2,1,0:T(8,128)} %shard_map.50), calls=%async_computation | async-start | bytes 1179648 | tf_op jit(solution)/shard_map/all_to_all | solution.py:416
  49.2 0.0 copy-start.6
  49.2 0.7 copy-done.6
  49.9 0.7 fusion.18
  51.9 0.6 compare_select_fusion.4
  52.5 1.2 %compare_and_fusion = (pred[128]{0:T(512)(128)(4,1)S(1)}, pred[128]{0:T(512)(128)(4,1)S(1)}) fusion(s32[]{:T(128)} %bitcast.11, s32[]{:T(128)} %bitcast.7), kind=kLoop, calls=%fused_computation.10 | loop fusion | flops 3328 | bytes 264 | tf_op jit(solution)/shard_map/jit(remainder)/and | solution.py:404
  53.8 0.6 compare_select_fusion
  54.4 12.8 %all-to-all-done.own_ref = f32[16,72,128]{2,1,0:T(8,128)S(1)} async-done(((f32[16,72,128]{2,1,0:T(8,128)}), f32[16,72,128]{2,1,0:T(8,128)S(1)}, u32[]{:S(2)}, u32[]{:S(2)}) %all-to-all-start) | async-done | bytes 589856 | tf_op jit(solution)/shard_map/all_to_all | solution.py:416
  67.2 0.0 copy-start.2
  67.2 0.1 collective-permute-start.6
  67.3 4.1 %collective-permute-start.5 = (f32[16,48,128]{2,1,0:T(8,128)S(1)}, f32[16,48,128]{2,1,0:T(8,128)S(1)}, u32[]{:S(2)}, u32[]{:S(2)}) collective-permute-start(f32[16,48,128]{2,1,0:T(8,128)S(1)} %slice.36), channel_id=1, source_target_pairs={{0,224},{32,0},{64,32},{96,64},{128,96},{160,128},{192,160},{224,1... | collective-permute-start | bytes 1179656 | tf_op jit(solution)/shard_map/ppermute | solution.py:418
  71.4 0.0 collective-permute-start.4
  71.4 1.3 %fusion.13 = (f32[1,1,2,128]{3,2,1,0:T(2,128)S(1)}, f32[1,1,2,128]{3,2,1,0:T(2,128)S(1)}) fusion(pred[128]{0:T(512)(128)(4,1)S(1)} %get-tuple-element.24, s32[128]{0:T(128)S(1)} %get-tuple-element.19, s32[128]{0:T(128)S(1)} %get-tuple-element.20, s32[128]{0:T(128)S(1)} %and_select_fusion.3, s32[]{:T(128)} %bitcast.6, f32[]{:T(128)S(6)} %div.37, ...), kind=kLoop, calls=%fused_computation.31 | loop fusion | flops 10496 | bytes 4888 | tf_op jit(solution)/shard_map/stack | solution.py:406
  72.8 0.1 fusion.15
  72.8 0.6 pad_maximum_fusion
  73.4 2.1 %shard_map.51.m_ref = f32[72,128]{1,0:T(8,128)} custom-call(s32[4]{0:T(128)} %pad_add_fusion.sc, f32[54,32,128]{2,1,0:T(8,128)} %bitcast.21, f32[808,128]{1,0:T(8,128)} %copy-done.1), custom_call_target="tpu_custom_call" | custom-call | flops 1048576 | bytes 1572864 | tf_op jit(solution)/shard_map/pallas_call | solution.py:394
  75.5 0.0 copy-done.2
  75.5 2.5 %collective-permute-done.6.behind_ref = f32[16,48,128]{2,1,0:T(8,128)S(1)} collective-permute-done((f32[16,48,128]{2,1,0:T(8,128)S(1)}, f32[16,48,128]{2,1,0:T(8,128)S(1)}, u32[]{:S(2)}, u32[]{:S(2)}) %collective-permute-start.6) | collective-permute-done | bytes 393248 | tf_op jit(solution)/shard_map/ppermute | solution.py:419
  78.0 0.0 copy-start.8
  78.0 0.0 collective-permute-done.5.ahead_ref
  78.0 0.0 copy-start.9
  78.0 0.0 collective-permute-done.4.other_ref
  78.0 0.0 copy-start.10
  78.0 0.7 copy-done.8
  78.7 0.2 copy-done.9
  78.9 0.1 copy-done.10
  79.0 4.2 %shard_map.52 = f32[8,64,128]{2,1,0:T(8,128)} custom-call(s32[4]{0:T(128)} %pad_add_fusion.sc, f32[16,72,128]{2,1,0:T(8,128)} %copy-done.2, f32[16,48,128]{2,1,0:T(8,128)} %copy-done.10, f32[16,48,128]{2,1,0:T(8,128)} %copy-done.9, f32[16,48,128]{2,1,0:T(8,128)} %copy-done.8, f32[72,128]{1,0:T(8,128)} %shard_map.51.m_ref, f32[8,128]{1,0:T(8,128)} %bitcast.31), custom_call_target="tpu_custom_call" | custom-call | flops 629145600 | bytes 2359296 | tf_op jit(solution)/shard_map/pallas_call | solution.py:422
  83.3 22.7 %all_to_all.10 = f32[128,4,128]{2,1,0:T(4,128)} all-to-all(f32[128,4,128]{2,1,0:T(4,128)} %bitcast.30), channel_id=1, replica_groups={{0,2,4,6,8,10,12,14,16,18,20,22,24,26,28,30,32,34,36,38,40,42,44,46,48,..., dimensions={0} | all-to-all | bytes 524288 | tf_op jit(solution)/shard_map/all_to_all | solution.py:433
  106.0 1.6 %shard_map.53 = f32[8,4,16]{2,1,0:T(4,128)} custom-call(f32[512,128]{1,0:T(8,128)} %bitcast.29), custom_call_target="tpu_custom_call" | custom-call | tf_op jit(solution)/shard_map/pallas_call | solution.py:434
  (3 shorter events, 0.0 us)
Async XLA Ops:
  1.7 0.7 copy-start.7
  3.0 3.7 %copy-start = (f32[2,3,4,1,4096]{4,3,2,1,0:T(1,128)S(1)}, f32[2,3,4,1,4096]{4,3,2,1,0:T(1,128)}, u32[]{:S(2)}) copy-start(f32[2,3,4,1,4096]{4,3,2,1,0:T(1,128)} %param.4) | copy-start | bytes 1179652
  5.0 13.6 %collective-permute-start.1 = (f32[808,128]{1,0:T(8,128)}, f32[808,128]{1,0:T(8,128)S(1)}, u32[]{:S(2)}, u32[]{:S(2)}) collective-permute-start(f32[808,128]{1,0:T(8,128)} %shard_map.47), channel_id=1, source_target_pairs={{0,32},{32,64},{64,96},{96,128},{128,160},{160,192},{192,224},{224... | collective-permute-start | bytes 1241096 | tf_op jit(solution)/shard_map/ppermute | solution.py:383
  6.6 10.7 %collective-permute-start = (f32[24,32,128]{2,1,0:T(8,128)S(1)}, f32[24,32,128]{2,1,0:T(8,128)S(1)}, u32[]{:S(2)}, u32[]{:S(2)}) collective-permute-start(f32[24,32,128]{2,1,0:T(8,128)S(1)} %bitcast.28), channel_id=1, source_target_pairs={{0,224},{32,0},{64,32},{96,64},{128,96},{160,128},{192,160},{224,1... | collective-permute-start | bytes 1179656 | tf_op jit(solution)/shard_map/ppermute | solution.py:377
  17.3 1.4 %copy-start.5 = (f32[24,32,128]{2,1,0:T(8,128)}, f32[24,32,128]{2,1,0:T(8,128)S(1)}, u32[]{:S(2)}) copy-start(f32[24,32,128]{2,1,0:T(8,128)S(1)} %collective-permute-done.ahead_ref) | copy-start | bytes 1179652
  18.7 0.8 copy-start.1
  22.0 12.3 %collective-permute-start.3 = (f32[24,32,128]{2,1,0:T(8,128)}, f32[24,32,128]{2,1,0:T(8,128)S(1)}, u32[]{:S(2)}, u32[]{:S(2)}) collective-permute-start(f32[24,32,128]{2,1,0:T(8,128)} %get-tuple-element.8), channel_id=1, source_target_pairs={{0,32},{32,64},{64,96},{96,128},{128,160},{160,192},{192,224},{224... | collective-permute-start | bytes 1179656 | tf_op jit(solution)/shard_map/ppermute | solution.py:392
  22.9 11.4 %collective-permute-start.2 = (f32[24,32,128]{2,1,0:T(8,128)}, f32[24,32,128]{2,1,0:T(8,128)S(1)}, u32[]{:S(2)}, u32[]{:S(2)}) collective-permute-start(f32[24,32,128]{2,1,0:T(8,128)} %get-tuple-element.7.v_ref), channel_id=1, source_target_pairs={{0,224},{32,0},{64,32},{96,64},{128,96},{160,128},{192,160},{224,1... | collective-permute-start | bytes 1179656 | tf_op jit(solution)/shard_map/ppermute | solution.py:391
  34.3 0.8 copy-start.3
  35.1 0.8 copy-start.4
  39.1 28.1 %all-to-all-start = ((f32[16,72,128]{2,1,0:T(8,128)}), f32[16,72,128]{2,1,0:T(8,128)S(1)}, u32[]{:S(2)}, u32[]{:S(2)}) async-start(f32[16,72,128]{2,1,0:T(8,128)} %shard_map.50), calls=%async_computation | async-start | bytes 1179648 | tf_op jit(solution)/shard_map/all_to_all | solution.py:416
  49.2 0.7 copy-start.6
  67.2 8.3 %copy-start.2 = (f32[16,72,128]{2,1,0:T(8,128)}, f32[16,72,128]{2,1,0:T(8,128)S(1)}, u32[]{:S(2)}) copy-start(f32[16,72,128]{2,1,0:T(8,128)S(1)} %all-to-all-done.own_ref) | copy-start | bytes 1769476
  67.2 10.8 %collective-permute-start.6 = (f32[16,48,128]{2,1,0:T(8,128)S(1)}, f32[16,48,128]{2,1,0:T(8,128)S(1)}, u32[]{:S(2)}, u32[]{:S(2)}) collective-permute-start(f32[16,48,128]{2,1,0:T(8,128)S(1)} %slice.36), channel_id=1, source_target_pairs={{0,32},{32,64},{64,96},{96,128},{128,160},{160,192},{192,224},{224... | collective-permute-start | bytes 1179656 | tf_op jit(solution)/shard_map/ppermute | solution.py:419
  67.3 10.7 %collective-permute-start.5 = (f32[16,48,128]{2,1,0:T(8,128)S(1)}, f32[16,48,128]{2,1,0:T(8,128)S(1)}, u32[]{:S(2)}, u32[]{:S(2)}) collective-permute-start(f32[16,48,128]{2,1,0:T(8,128)S(1)} %slice.36), channel_id=1, source_target_pairs={{0,224},{32,0},{64,32},{96,64},{128,96},{160,128},{192,160},{224,1... | collective-permute-start | bytes 1179656 | tf_op jit(solution)/shard_map/ppermute | solution.py:418
  71.4 6.6 %collective-permute-start.4 = (f32[16,48,128]{2,1,0:T(8,128)S(1)}, f32[16,48,128]{2,1,0:T(8,128)S(1)}, u32[]{:S(2)}, u32[]{:S(2)}) collective-permute-start(f32[16,48,128]{2,1,0:T(8,128)S(1)} %slice.36), channel_id=1, source_target_pairs={{0,1},{1,0},{2,3},{3,2},{4,5},{5,4},{6,7},{7,6},{8,9},{9,8},{10,11... | collective-permute-start | bytes 1179656 | tf_op jit(solution)/shard_map/ppermute | solution.py:420
  78.0 0.7 copy-start.8
  78.0 0.9 copy-start.9
  78.0 1.1 copy-start.10

commit v2 on v1

--- a/solution.py
+++ b/solution.py
@@ -18,20 +18,28 @@
 F32 = jnp.float32
 
 
-def call(body, out_shape, n_in, scratch=(), scalars=False, flops=0, nbytes=0):
-    specs = [pl.BlockSpec(memory_space=VMEM)] * n_in
-    if scalars:
-        specs = [pl.BlockSpec(memory_space=pltpu.SMEM)] + specs
+LINKS = pl.BlockSpec((18, ROWS, LANES), lambda i: (0, 0, 0))
+
+
+def call(body, out_shape, ins, scratch=(), flops=0, nbytes=0, room=8):
+    kinds = {
+        "s": pl.BlockSpec(memory_space=pltpu.SMEM),
+        "x": LINKS,
+        "v": pl.BlockSpec(memory_space=VMEM),
+    }
+    specs = [kinds[letter] for letter in ins]
     many = isinstance(out_shape, (list, tuple))
     return pl.pallas_call(
         body,
         out_shape=out_shape,
+        grid=(1,) if "x" in ins else (),
         in_specs=specs,
         out_specs=[pl.BlockSpec(memory_space=VMEM)] * len(out_shape)
         if many
         else pl.BlockSpec(memory_space=VMEM),
         scratch_shapes=list(scratch),
         cost_estimate=pl.CostEstimate(flops=flops, bytes_accessed=nbytes, transcendentals=0),
+        compiler_params=pltpu.CompilerParams(vmem_limit_bytes=room << 20),
     )
 
 
@@ -97,7 +105,7 @@
     return lambda reim, row, col: g_ref[direction * 18 + reim * 9 + row * 3 + col]
 
 
-def start_body(sc, v_ref, g_ref, w_ref):
+def start_body(v_ref, g_ref, w_ref):
     link = plane_link(g_ref, 0)
 
     def one(n, carry):
@@ -107,7 +115,7 @@
         return carry
 
     lax.fori_loop(0, 4, one, 0)
-    block = sc[0]
+    block = lax.axis_index("vec") // 2
     for n in range(18):
         w_ref[24 * ROWS + 2 * n : 24 * ROWS + 2 * n + 2, :] = g_ref[n, pl.ds(2 * block, 2), :]
     w_ref[24 * ROWS + 36 :, :] = jnp.zeros((4, LANES), F32)
@@ -173,10 +181,10 @@
 
 
 def matrix_body(sc, g_ref, behind_ref, m_ref):
-    block = sc[0]
+    block = lax.axis_index("vec") // 2
     low = lane_of((1, LANES)) < NZ
     for op in range(NDISP):
-        hop = lax.rem(sc[2 + op] + 3, 6)
+        hop = lax.rem(sc[op] + 3, 6)
         direction = lax.rem(hop, 3)
 
         def put(reim, row, col, q, value):
@@ -237,7 +245,7 @@
     scale, sc, own_ref, other_ref, ahead_ref, behind_ref, m_ref, ph_ref, out_ref,
     f_ref, n_ref, lhs_hi, lhs_lo, rhs_hi, rhs_lo,
 ):
-    core = sc[1]
+    core = lax.rem(lax.axis_index("vec"), 2)
 
     def column(k, q):
         return slice((2 * k + q) * LANES, (2 * k + q + 1) * LANES)
@@ -277,7 +285,7 @@
                 put_lhs(op, 3 + c, q, cosine * im - sine * re)
     low = lane_of((64, LANES)) < NZ
     for op in range(NDISP):
-        hop = lax.rem(sc[2 + op] + 3, 6)
+        hop = lax.rem(sc[op] + 3, 6)
 
         for which, ref in ((0, ahead_ref), (3, behind_ref)):
 
@@ -364,10 +372,6 @@
     gauge = gauge_links.reshape(54, ROWS, LANES)
     slab = lax.axis_index("space")
     block = lax.axis_index("vec") // 2
-    core = lax.axis_index("vec") % 2
-    scalars = jnp.concatenate(
-        [jnp.stack([block, core]).astype(jnp.int32), displacements.astype(jnp.int32)]
-    )
     up = [(i, (i + 1) % slabs) for i in range(slabs)]
     down = [(i, (i - 1) % slabs) for i in range(slabs)]
     partner = [(i, i ^ 1) for i in range(vecs)]
@@ -376,24 +380,21 @@
 
     ahead = lax.ppermute(field, "space", down)
     shape = struct(24 * ROWS + 40, LANES)
-    gauge_x = gauge[:18]
-    w = call(start_body, shape, 2, scalars=True, flops=3 << 20, nbytes=3 * field_bytes)(
-        scalars, field, gauge_x
-    )
+    w = call(start_body, shape, "vx", flops=3 << 20, nbytes=3 * field_bytes)(field, gauge)
     behind = lax.ppermute(w, "space", up)
     inner = call(
-        inner_body, struct(24, ROWS, LANES), 2, flops=12 << 20, nbytes=5 * field_bytes
+        inner_body, struct(24, ROWS, LANES), "vv", flops=12 << 20, nbytes=5 * field_bytes
     )
     acc = inner(field, gauge)
     first, w = call(
-        first_body, [struct(24, ROWS, LANES)] * 2, 4, flops=6 << 20, nbytes=6 * field_bytes
-    )(acc, ahead, behind, gauge_x)
+        first_body, [struct(24, ROWS, LANES)] * 2, "vvvx", flops=6 << 20, nbytes=6 * field_bytes
+    )(acc, ahead, behind, gauge)
     ahead2 = lax.ppermute(first, "space", down)
     behind2 = lax.ppermute(w, "space", up)
     acc = inner(first, gauge)
     matrices = call(
-        matrix_body, struct(72, LANES), 2, scalars=True, flops=1 << 20, nbytes=4 * field_bytes
-    )(scalars, gauge, behind)
+        matrix_body, struct(72, LANES), "svv", flops=1 << 20, nbytes=4 * field_bytes
+    )(displacements, gauge, behind)
     lane = jnp.arange(LANES, dtype=jnp.int32)
     row = 4 * block + 2 * jnp.arange(2, dtype=jnp.int32)[:, None] + lane[None, :] // NZ
     depth = jnp.broadcast_to(lane % NZ, row.shape)
@@ -408,11 +409,11 @@
     cut = call(
         second_body,
         struct(16, 72, LANES),
-        5,
+        "vvvvx",
         scratch=[VMEM((24 * ROWS, LANES), F32)] * 2,
         flops=6 << 20,
         nbytes=7 * field_bytes,
-    )(acc, ahead2, behind2, field, gauge_x)
+    )(acc, ahead2, behind2, field, gauge)
     own = lax.all_to_all(cut, "vec", 0, 0, axis_index_groups=cores)
     bulk = own[:, :48]
     ahead3 = lax.ppermute(bulk, "space", down)
@@ -422,16 +423,16 @@
     sums = call(
         functools.partial(gram_body, scale),
         struct(slabs, 64, LANES),
-        6,
+        "svvvvvv",
         scratch=[VMEM((6, 2, 64, LANES), F32)] * 2
         + [VMEM((256, 12 * LANES), jnp.bfloat16)] * 4,
-        scalars=True,
+        room=16,
         flops=600 << 20,
         nbytes=6 * field_bytes,
-    )(scalars, own, other, ahead3, behind3, matrices, phases)
+    )(displacements, own, other, ahead3, behind3, matrices, phases)
     sums = sums.reshape(slabs * vecs // 2, 4, LANES)
     parts = lax.all_to_all(sums, ("space", "vec"), 0, 0, axis_index_groups=alike)
-    out = call(finish_body, struct(8, 4, 16), 1)(parts.reshape(512, LANES))
+    out = call(finish_body, struct(8, 4, 16), "v")(parts.reshape(512, LANES))
     return out.reshape(2, 4, 4, 16)
 
 

time: 108 us -> 95.6 us (0.89)
  Pallas kernels: 22 us -> 8.84 us
  waiting for transfers between devices: 26.7 us -> 31.6 us
  local copies, waits for them, and re-layouts: 7.02 us -> 4.16 us
  other arithmetic: 5.11 us -> 3.92 us
    pallas_call x6, Pallas kernels: 15.9 us -> 6.78 us  [the longest x1 2.83 us: local(): call(functools.partial(gram_body, scale), struct(slabs, 64, LANES), 'svvv...]
    pallas_call x1, Pallas kernels: 3.06 us -> 1.01 us  [local(): acc = inner(field, gauge)]
    ppermute x1, waiting for transfers between devices: 5.03 us -> 7.07 us  [local(): ahead = lax.ppermute(field, 'space', down)]
    pallas_call x1, Pallas kernels: 3.06 us -> 1.05 us  [local(): acc = inner(first, gauge)]
    ppermute x1, waiting for transfers between devices: 5.11 us -> 6.9 us  [local(): behind2 = lax.ppermute(w, 'space', up)]
    slice x1 -> x0, local copies, waits for them, and re-layouts: 1.7 us -> none  [local(): gauge_x = gauge[:18]]
    unnamed x22 -> x10, local copies, waits for them, and re-layouts: 4.65 us -> 3.48 us
  transfers between devices with their start and end apart: 8 -> 8, of which waited for: 5 -> 5; matrix products, arithmetic and copies ran while one was open for 5% -> 5% of each run, Pallas kernels for 8% -> 3%
where the time goes in v2:
time: 95.6 us; the launch traced here: 95.3 us
  waiting for transfers between devices  31.6 us (33%)
  starting transfers between devices  22.8 us (24%)
  blocking collectives  22.5 us (24%)
  Pallas kernels  8.84 us (9%)
  local copies, waits for them, and re-layouts  4.16 us (4%)
  other arithmetic  3.92 us (4%)
  between operations  1.49 us (2%)
    all_to_all x1, blocking collectives, local(): lax.all_to_all(sums, ('space', 'vec'), 0, 0, axis_index_groups=alike)  22.5 us
    all_to_all x1, waiting for transfers between devices, local(): own = lax.all_to_all(cut, 'vec', 0, 0, axis_index_groups=cores)  12.9 us
    all_to_all x1, starting transfers between devices, local(): own = lax.all_to_all(cut, 'vec', 0, 0, axis_index_groups=cores)  10.1 us
    ppermute x1, waiting for transfers between devices, local(): ahead = lax.ppermute(field, 'space', down)  7.07 us
    ppermute x1, waiting for transfers between devices, local(): behind2 = lax.ppermute(w, 'space', up)  6.9 us
    ppermute x1, starting transfers between devices, local(): ahead3 = lax.ppermute(bulk, 'space', down)  4.12 us
    ppermute x1, starting transfers between devices, local(): ahead2 = lax.ppermute(first, 'space', down)  3.81 us
    ppermute x1, waiting for transfers between devices, local(): behind3 = lax.ppermute(bulk, 'space', up)  3.53 us
  transfers between devices with their start and end apart: 8, of which 5 were waited for; matrix products, arithmetic and copies ran while one was open for 5% of the time, Pallas kernels for 3%

profile of v2, /device:TPU:32, one launch (start us, length us, event | category | flops | bytes accessed | tf_op | source)
XLA Modules:
  0.0 95.3 jit_solution(10731124758988865768)
XLA Ops:
  0.0 0.0 copy-start
  0.0 1.2 %copy-done = f32[3,2,3,3,1,4096]{5,4,3,2,1,0:T(1,128)S(1)} copy-done((f32[3,2,3,3,1,4096]{5,4,3,2,1,0:T(1,128)S(1)}, f32[3,2,3,3,1,4096]{5,4,3,2,1,0:T(1,128)}, u32[]{:S(2)}) %copy-start) | copy-done | bytes 884760
  1.2 0.0 copy-start.2
  1.2 1.0 %copy-done.2 = f32[2,3,4,1,4096]{4,3,2,1,0:T(1,128)S(1)} copy-done((f32[2,3,4,1,4096]{4,3,2,1,0:T(1,128)S(1)}, f32[2,3,4,1,4096]{4,3,2,1,0:T(1,128)}, u32[]{:S(2)}) %copy-start.2) | copy-done | bytes 393240
  2.2 0.2 shard_map.47
  2.4 0.0 copy-start.1
  2.4 1.7 %collective-permute-start.1 = (f32[808,128]{1,0:T(8,128)S(1)}, f32[808,128]{1,0:T(8,128)S(1)}, u32[]{:S(2)}, u32[]{:S(2)}) collective-permute-start(f32[808,128]{1,0:T(8,128)S(1)} %shard_map.47), channel_id=1, source_target_pairs={{0,32},{32,64},{64,96},{96,128},{128,160},{160,192},{192,224},{224... | collective-permute-start | bytes 1241096 | tf_op jit(solution)/shard_map/ppermute | solution.py:384
  4.0 2.6 %collective-permute-start = (f32[24,32,128]{2,1,0:T(8,128)S(1)}, f32[24,32,128]{2,1,0:T(8,128)S(1)}, u32[]{:S(2)}, u32[]{:S(2)}) collective-permute-start(f32[24,32,128]{2,1,0:T(8,128)S(1)} %bitcast.23), channel_id=1, source_target_pairs={{0,224},{32,0},{64,32},{96,64},{128,96},{160,128},{192,160},{224,1... | collective-permute-start | bytes 1179656 | tf_op jit(solution)/shard_map/ppermute | solution.py:381
  6.6 1.0 %shard_map.46.acc_ref = f32[24,32,128]{2,1,0:T(8,128)S(1)} custom-call(f32[24,32,128]{2,1,0:T(8,128)S(1)} %bitcast.24, f32[54,32,128]{2,1,0:T(8,128)S(1)} %bitcast.17), custom_call_target="tpu_custom_call" | custom-call | flops 12582912 | bytes 1966080 | tf_op jit(solution)/shard_map/pallas_call | solution.py:388
  7.6 7.1 %collective-permute-done.ahead_ref = f32[24,32,128]{2,1,0:T(8,128)S(1)} collective-permute-done((f32[24,32,128]{2,1,0:T(8,128)S(1)}, f32[24,32,128]{2,1,0:T(8,128)S(1)}, u32[]{:S(2)}, u32[]{:S(2)}) %collective-permute-start) | collective-permute-done | bytes 393248 | tf_op jit(solution)/shard_map/ppermute | solution.py:381
  14.7 1.2 %collective-permute-done.1.behind_ref = f32[808,128]{1,0:T(8,128)S(1)} collective-permute-done((f32[808,128]{1,0:T(8,128)S(1)}, f32[808,128]{1,0:T(8,128)S(1)}, u32[]{:S(2)}, u32[]{:S(2)}) %collective-permute-start.1) | collective-permute-done | bytes 413728 | tf_op jit(solution)/shard_map/ppermute | solution.py:384
  15.9 0.0 copy-done.1
  15.9 0.4 shard_map.48
  16.3 0.4 collective-permute-start.3
  16.7 3.8 %collective-permute-start.2 = (f32[24,32,128]{2,1,0:T(8,128)S(1)}, f32[24,32,128]{2,1,0:T(8,128)S(1)}, u32[]{:S(2)}, u32[]{:S(2)}) collective-permute-start(f32[24,32,128]{2,1,0:T(8,128)S(1)} %get-tuple-element.7.v_ref), channel_id=1, source_target_pairs={{0,224},{32,0},{64,32},{96,64},{128,96},{160,128},{192,160},{224,1... | collective-permute-start | bytes 1179656 | tf_op jit(solution)/shard_map/ppermute | solution.py:392
  20.5 1.0 %shard_map.49.acc_ref = f32[24,32,128]{2,1,0:T(8,128)S(1)} custom-call(f32[24,32,128]{2,1,0:T(8,128)S(1)} %get-tuple-element.7.v_ref, f32[54,32,128]{2,1,0:T(8,128)S(1)} %bitcast.19), custom_call_target="tpu_custom_call" | custom-call | flops 12582912 | bytes 1966080 | tf_op jit(solution)/shard_map/pallas_call | solution.py:394
  21.6 6.9 %collective-permute-done.3.behind_ref = f32[24,32,128]{2,1,0:T(8,128)S(1)} collective-permute-done((f32[24,32,128]{2,1,0:T(8,128)S(1)}, f32[24,32,128]{2,1,0:T(8,128)S(1)}, u32[]{:S(2)}, u32[]{:S(2)}) %collective-permute-start.3) | collective-permute-done | bytes 393248 | tf_op jit(solution)/shard_map/ppermute | solution.py:393
  28.5 0.0 collective-permute-done.2.ahead_ref
  28.5 1.8 %shard_map.50 = f32[16,72,128]{2,1,0:T(8,128)} custom-call(f32[24,32,128]{2,1,0:T(8,128)S(1)} %shard_map.49.acc_ref, f32[24,32,128]{2,1,0:T(8,128)S(1)} %collective-permute-done.2.ahead_ref, f32[24,32,128]{2,1,0:T(8,128)S(1)} %collective-permute-done.3.behind_ref, f32[24,32,128]{2,1,0:T(8,128)S(1)} %bitcast.25, f32[54,32,128]{2,1,0:T(8,128)S(1)} %bitcast.20), custom_call_target="tpu_custom_call" | custom-call | flops 6291456 | bytes 2752512 | tf_op jit(solution)/shard_map/pallas_call | solution.py:409
  30.3 10.1 %all-to-all-start = ((f32[16,72,128]{2,1,0:T(8,128)}), f32[16,72,128]{2,1,0:T(8,128)S(1)}, u32[]{:S(2)}, u32[]{:S(2)}) async-start(f32[16,72,128]{2,1,0:T(8,128)} %shard_map.50), calls=%async_computation | async-start | bytes 1179648 | tf_op jit(solution)/shard_map/all_to_all | solution.py:417
  40.4 0.0 copy-start.4
  40.4 0.7 copy-done.4
  41.1 0.7 fusion.18
  43.1 0.7 compare_select_fusion.4
  43.8 1.2 %compare_and_fusion = (pred[128]{0:T(512)(128)(4,1)S(1)}, pred[128]{0:T(512)(128)(4,1)S(1)}) fusion(s32[]{:T(128)} %bitcast.8, s32[]{:T(128)} %bitcast.4), kind=kLoop, calls=%fused_computation.10 | loop fusion | flops 3328 | bytes 264 | tf_op jit(solution)/shard_map/jit(remainder)/and | solution.py:405
  45.0 0.6 compare_select_fusion
  45.6 12.9 %all-to-all-done.own_ref = f32[16,72,128]{2,1,0:T(8,128)S(1)} async-done(((f32[16,72,128]{2,1,0:T(8,128)}), f32[16,72,128]{2,1,0:T(8,128)S(1)}, u32[]{:S(2)}, u32[]{:S(2)}) %all-to-all-start) | async-done | bytes 589856 | tf_op jit(solution)/shard_map/all_to_all | solution.py:417
  58.5 0.1 collective-permute-start.6
  58.6 4.1 %collective-permute-start.5 = (f32[16,48,128]{2,1,0:T(8,128)S(1)}, f32[16,48,128]{2,1,0:T(8,128)S(1)}, u32[]{:S(2)}, u32[]{:S(2)}) collective-permute-start(f32[16,48,128]{2,1,0:T(8,128)S(1)} %slice.28), channel_id=1, source_target_pairs={{0,224},{32,0},{64,32},{96,64},{128,96},{160,128},{192,160},{224,1... | collective-permute-start | bytes 1179656 | tf_op jit(solution)/shard_map/ppermute | solution.py:419
  62.7 0.0 collective-permute-start.4
  62.7 1.4 %fusion.13 = (f32[1,1,2,128]{3,2,1,0:T(2,128)S(1)}, f32[1,1,2,128]{3,2,1,0:T(2,128)S(1)}) fusion(pred[128]{0:T(512)(128)(4,1)S(1)} %get-tuple-element.24, s32[128]{0:T(128)S(1)} %get-tuple-element.19, s32[128]{0:T(128)S(1)} %get-tuple-element.20, s32[128]{0:T(128)S(1)} %and_select_fusion.3, s32[]{:T(128)} %bitcast.3, f32[]{:T(128)S(6)} %div.34, ...), kind=kLoop, calls=%fused_computation.31 | loop fusion | flops 10496 | bytes 4888 | tf_op jit(solution)/shard_map/stack | solution.py:407
  64.1 0.1 fusion.15
  64.2 0.0 copy-start.3
  64.2 0.6 copy-done.3
  64.8 0.8 shard_map.51.m_ref
  65.7 3.5 %collective-permute-done.6.behind_ref = f32[16,48,128]{2,1,0:T(8,128)S(1)} collective-permute-done((f32[16,48,128]{2,1,0:T(8,128)S(1)}, f32[16,48,128]{2,1,0:T(8,128)S(1)}, u32[]{:S(2)}, u32[]{:S(2)}) %collective-permute-start.6) | collective-permute-done | bytes 393248 | tf_op jit(solution)/shard_map/ppermute | solution.py:420
  69.2 0.0 collective-permute-done.5.ahead_ref
  69.2 0.0 collective-permute-done.4.other_ref
  69.2 2.8 %shard_map.52 = f32[8,64,128]{2,1,0:T(8,128)S(1)} custom-call(s32[2]{0:T(128)S(1)} %copy-done.3, f32[16,72,128]{2,1,0:T(8,128)S(1)} %all-to-all-done.own_ref, f32[16,48,128]{2,1,0:T(8,128)S(1)} %collective-permute-done.4.other_ref, f32[16,48,128]{2,1,0:T(8,128)S(1)} %collective-permute-done.5.ahead_ref, ...), custom_call_target="tpu_custom_call" | custom-call | flops 629145600 | bytes 2359296 | tf_op jit(solution)/shard_map/pallas_call | solution.py:423
  72.0 22.5 %all_to_all.10 = f32[128,4,128]{2,1,0:T(4,128)S(1)} all-to-all(f32[128,4,128]{2,1,0:T(4,128)S(1)} %bitcast.27), channel_id=1, replica_groups={{0,2,4,6,8,10,12,14,16,18,20,22,24,26,28,30,32,34,36,38,40,42,44,46,48,..., dimensions={0} | all-to-all | bytes 524288 | tf_op jit(solution)/shard_map/all_to_all | solution.py:434
  94.6 0.7 shard_map.53
  (4 shorter events, 0.0 us)
Async XLA Ops:
  0.0 1.2 %copy-start = (f32[3,2,3,3,1,4096]{5,4,3,2,1,0:T(1,128)S(1)}, f32[3,2,3,3,1,4096]{5,4,3,2,1,0:T(1,128)}, u32[]{:S(2)}) copy-start(f32[3,2,3,3,1,4096]{5,4,3,2,1,0:T(1,128)} %param.5) | copy-start | bytes 2654212
  1.2 1.0 %copy-start.2 = (f32[2,3,4,1,4096]{4,3,2,1,0:T(1,128)S(1)}, f32[2,3,4,1,4096]{4,3,2,1,0:T(1,128)}, u32[]{:S(2)}) copy-start(f32[2,3,4,1,4096]{4,3,2,1,0:T(1,128)} %param.4) | copy-start | bytes 1179652
  2.4 13.5 %copy-start.1 = (f32[3,2,3,3,1,4096]{5,4,3,2,1,0:T(1,128)S(1)}, f32[3,2,3,3,1,4096]{5,4,3,2,1,0:T(1,128)}, u32[]{:S(2)}) copy-start(f32[3,2,3,3,1,4096]{5,4,3,2,1,0:T(1,128)} %param.5) | copy-start | bytes 2654212
  2.4 13.5 %collective-permute-start.1 = (f32[808,128]{1,0:T(8,128)S(1)}, f32[808,128]{1,0:T(8,128)S(1)}, u32[]{:S(2)}, u32[]{:S(2)}) collective-permute-start(f32[808,128]{1,0:T(8,128)S(1)} %shard_map.47), channel_id=1, source_target_pairs={{0,32},{32,64},{64,96},{96,128},{128,160},{160,192},{192,224},{224... | collective-permute-start | bytes 1241096 | tf_op jit(solution)/shard_map/ppermute | solution.py:384
  4.0 10.7 %collective-permute-start = (f32[24,32,128]{2,1,0:T(8,128)S(1)}, f32[24,32,128]{2,1,0:T(8,128)S(1)}, u32[]{:S(2)}, u32[]{:S(2)}) collective-permute-start(f32[24,32,128]{2,1,0:T(8,128)S(1)} %bitcast.23), channel_id=1, source_target_pairs={{0,224},{32,0},{64,32},{96,64},{128,96},{160,128},{192,160},{224,1... | collective-permute-start | bytes 1179656 | tf_op jit(solution)/shard_map/ppermute | solution.py:381
  16.3 12.2 %collective-permute-start.3 = (f32[24,32,128]{2,1,0:T(8,128)S(1)}, f32[24,32,128]{2,1,0:T(8,128)S(1)}, u32[]{:S(2)}, u32[]{:S(2)}) collective-permute-start(f32[24,32,128]{2,1,0:T(8,128)S(1)} %get-tuple-element.8), channel_id=1, source_target_pairs={{0,32},{32,64},{64,96},{96,128},{128,160},{160,192},{192,224},{224... | collective-permute-start | bytes 1179656 | tf_op jit(solution)/shard_map/ppermute | solution.py:393
  16.7 11.8 %collective-permute-start.2 = (f32[24,32,128]{2,1,0:T(8,128)S(1)}, f32[24,32,128]{2,1,0:T(8,128)S(1)}, u32[]{:S(2)}, u32[]{:S(2)}) collective-permute-start(f32[24,32,128]{2,1,0:T(8,128)S(1)} %get-tuple-element.7.v_ref), channel_id=1, source_target_pairs={{0,224},{32,0},{64,32},{96,64},{128,96},{160,128},{192,160},{224,1... | collective-permute-start | bytes 1179656 | tf_op jit(solution)/shard_map/ppermute | solution.py:392
  30.3 28.2 %all-to-all-start = ((f32[16,72,128]{2,1,0:T(8,128)}), f32[16,72,128]{2,1,0:T(8,128)S(1)}, u32[]{:S(2)}, u32[]{:S(2)}) async-start(f32[16,72,128]{2,1,0:T(8,128)} %shard_map.50), calls=%async_computation | async-start | bytes 1179648 | tf_op jit(solution)/shard_map/all_to_all | solution.py:417
  40.4 0.7 copy-start.4
  58.5 10.7 %collective-permute-start.6 = (f32[16,48,128]{2,1,0:T(8,128)S(1)}, f32[16,48,128]{2,1,0:T(8,128)S(1)}, u32[]{:S(2)}, u32[]{:S(2)}) collective-permute-start(f32[16,48,128]{2,1,0:T(8,128)S(1)} %slice.28), channel_id=1, source_target_pairs={{0,32},{32,64},{64,96},{96,128},{128,160},{160,192},{192,224},{224... | collective-permute-start | bytes 1179656 | tf_op jit(solution)/shard_map/ppermute | solution.py:420
  58.6 10.6 %collective-permute-start.5 = (f32[16,48,128]{2,1,0:T(8,128)S(1)}, f32[16,48,128]{2,1,0:T(8,128)S(1)}, u32[]{:S(2)}, u32[]{:S(2)}) collective-permute-start(f32[16,48,128]{2,1,0:T(8,128)S(1)} %slice.28), channel_id=1, source_target_pairs={{0,224},{32,0},{64,32},{96,64},{128,96},{160,128},{192,160},{224,1... | collective-permute-start | bytes 1179656 | tf_op jit(solution)/shard_map/ppermute | solution.py:419
  62.7 6.5 %collective-permute-start.4 = (f32[16,48,128]{2,1,0:T(8,128)S(1)}, f32[16,48,128]{2,1,0:T(8,128)S(1)}, u32[]{:S(2)}, u32[]{:S(2)}) collective-permute-start(f32[16,48,128]{2,1,0:T(8,128)S(1)} %slice.28), channel_id=1, source_target_pairs={{0,1},{1,0},{2,3},{3,2},{4,5},{5,4},{6,7},{7,6},{8,9},{9,8},{10,11... | collective-permute-start | bytes 1179656 | tf_op jit(solution)/shard_map/ppermute | solution.py:421
  64.2 0.7 copy-start.3

commit v3 on v2

--- a/solution.py
+++ b/solution.py
@@ -158,7 +158,7 @@
     lax.fori_loop(0, 4, one, 0)
 
 
-def second_body(acc_ref, ahead_ref, behind_ref, v_ref, g_ref, out_ref, f_ref, half_ref):
+def second_body(edges, acc_ref, ahead_ref, behind_ref, v_ref, g_ref, out_ref, f_ref, half_ref):
     link = plane_link(g_ref, 0)
 
     def one(n, carry):
@@ -167,7 +167,8 @@
             r = 4 * k + n
             f = (acc_ref[r] + hop[k] + behind_ref[r]) / -3.0 - v_ref[r]
             f_ref[pl.ds(r * ROWS, ROWS), :] = f
-            half_ref[pl.ds(r * ROWS, ROWS), :] = pltpu.roll(f, NZ, 1)
+            if edges:
+                half_ref[pl.ds(r * ROWS, ROWS), :] = pltpu.roll(f, NZ, 1)
         return carry
 
     lax.fori_loop(0, 4, one, 0)
@@ -175,6 +176,8 @@
     for block in range(16):
         for q in range(2):
             out_ref[block, 24 * q : 24 * q + 24, :] = f_ref[pl.ds(2 * block + q, 24, ROWS), :]
+        if not edges:
+            continue
         under = half_ref[pl.ds((2 * block - 1) % ROWS, 24, ROWS), :]
         over = half_ref[pl.ds((2 * block + 2) % ROWS, 24, ROWS), :]
         out_ref[block, 48:72, :] = jnp.where(low, under, over)
@@ -242,7 +245,7 @@
 
 
 def gram_body(
-    scale, sc, own_ref, other_ref, ahead_ref, behind_ref, m_ref, ph_ref, out_ref,
+    scale, along_x, along_y, sc, own_ref, other_ref, ahead_ref, behind_ref, m_ref, ph_ref, out_ref,
     f_ref, n_ref, lhs_hi, lhs_lo, rhs_hi, rhs_lo,
 ):
     core = lax.rem(lax.axis_index("vec"), 2)
@@ -287,7 +290,7 @@
     for op in range(NDISP):
         hop = lax.rem(sc[op] + 3, 6)
 
-        for which, ref in ((0, ahead_ref), (3, behind_ref)):
+        for which, ref in ((0, ahead_ref), (3, behind_ref)) if along_x else ():
 
             @pl.when(hop == which)
             def _():
@@ -295,21 +298,23 @@
                     for q in range(2):
                         n_ref[k, q] = rows_of_block(ref, 3 * q + k // 2, k % 2)
 
-        @pl.when(hop == 1)
-        def _():
+        def y_ahead():
             for k in range(6):
                 edge = rows_of_block(own_ref, 6 + k // 2, k % 2)
                 here, over = pltpu.roll(f_ref[k, 0], NZ, 1), pltpu.roll(f_ref[k, 1], NZ, 1)
                 n_ref[k, 0] = jnp.where(low, here, over)
                 n_ref[k, 1] = jnp.where(low, over, edge)
 
-        @pl.when(hop == 4)
-        def _():
+        def y_behind():
             for k in range(6):
                 edge = rows_of_block(own_ref, 6 + k // 2, k % 2)
                 here, over = pltpu.roll(f_ref[k, 0], NZ, 1), pltpu.roll(f_ref[k, 1], NZ, 1)
                 n_ref[k, 0] = jnp.where(low, edge, here)
                 n_ref[k, 1] = jnp.where(low, here, over)
+
+        if along_y:
+            pl.when(hop == 1)(y_ahead)
+            pl.when(hop == 4)(y_behind)
 
         @pl.when(hop == 2)
         def _():
@@ -378,10 +383,11 @@
     cores = [[2 * i + c for i in range(vecs // 2)] for c in range(2)]
     alike = [[2 * i + c for i in range(slabs * vecs // 2)] for c in range(2)]
 
-    ahead = lax.ppermute(field, "space", down)
     shape = struct(24 * ROWS + 40, LANES)
     w = call(start_body, shape, "vx", flops=3 << 20, nbytes=3 * field_bytes)(field, gauge)
+    first_out, w = lax.optimization_barrier((field, w))
     behind = lax.ppermute(w, "space", up)
+    ahead = lax.ppermute(first_out, "space", down)
     inner = call(
         inner_body, struct(24, ROWS, LANES), "vv", flops=12 << 20, nbytes=5 * field_bytes
     )
@@ -406,33 +412,49 @@
         angles.append((part_x + part_y + part_z) * (2.0 * math.pi))
     angle = jnp.stack(angles)
     phases = jnp.stack([jnp.cos(angle), jnp.sin(angle)], axis=1).reshape(8, LANES)
-    cut = call(
-        second_body,
-        struct(16, 72, LANES),
-        "vvvvx",
-        scratch=[VMEM((24 * ROWS, LANES), F32)] * 2,
-        flops=6 << 20,
-        nbytes=7 * field_bytes,
-    )(acc, ahead2, behind2, field, gauge)
-    own = lax.all_to_all(cut, "vec", 0, 0, axis_index_groups=cores)
-    bulk = own[:, :48]
-    ahead3 = lax.ppermute(bulk, "space", down)
-    behind3 = lax.ppermute(bulk, "space", up)
-    other = lax.ppermute(bulk, "vec", partner)
+    along = displacements % 3
+    case = jnp.any(along == 0).astype(jnp.int32) + 2 * jnp.any(along == 1).astype(jnp.int32)
+    acc, phases, matrices, case = lax.optimization_barrier((acc, phases, matrices, case))
     scale = 1.0 / math.sqrt(3 * slabs * NY * NZ)
-    sums = call(
-        functools.partial(gram_body, scale),
-        struct(slabs, 64, LANES),
-        "svvvvvv",
-        scratch=[VMEM((6, 2, 64, LANES), F32)] * 2
-        + [VMEM((256, 12 * LANES), jnp.bfloat16)] * 4,
-        room=16,
-        flops=600 << 20,
-        nbytes=6 * field_bytes,
-    )(displacements, own, other, ahead3, behind3, matrices, phases)
-    sums = sums.reshape(slabs * vecs // 2, 4, LANES)
-    parts = lax.all_to_all(sums, ("space", "vec"), 0, 0, axis_index_groups=alike)
-    out = call(finish_body, struct(8, 4, 16), "v")(parts.reshape(512, LANES))
+
+    def elementals(along_x, along_y, acc, ahead2, behind2, field, gauge, phases, matrices):
+        cut = call(
+            functools.partial(second_body, along_y),
+            struct(16, 72 if along_y else 48, LANES),
+            "vvvvx",
+            scratch=[VMEM((24 * ROWS, LANES), F32)] * 2,
+            flops=6 << 20,
+            nbytes=7 * field_bytes,
+        )(acc, ahead2, behind2, field, gauge)
+        own = lax.all_to_all(cut, "vec", 0, 0, axis_index_groups=cores)
+        bulk = own[:, :48]
+        ahead3 = behind3 = bulk
+        if along_x:
+            ahead3 = lax.ppermute(bulk, "space", down)
+            behind3 = lax.ppermute(bulk, "space", up)
+        other = lax.ppermute(bulk, "vec", partner)
+        sums = call(
+            functools.partial(gram_body, scale, along_x, along_y),
+            struct(slabs, 64, LANES),
+            "svvvvvv",
+            scratch=[VMEM((6, 2, 64, LANES), F32)] * 2
+            + [VMEM((256, 12 * LANES), jnp.bfloat16)] * 4,
+            room=16,
+            flops=600 << 20,
+            nbytes=6 * field_bytes,
+        )(displacements, own, other, ahead3, behind3, matrices, phases)
+        sums = sums.reshape(slabs * vecs // 2, 4, LANES)
+        parts = lax.all_to_all(sums, ("space", "vec"), 0, 0, axis_index_groups=alike)
+        return call(finish_body, struct(8, 4, 16), "v")(parts.reshape(512, LANES))
+
+    out = lax.switch(
+        case,
+        [
+            functools.partial(elementals, bool(i & 1), bool(i & 2))
+            for i in range(4)
+        ],
+        acc, ahead2, behind2, field, gauge, phases, matrices,
+    )
     return out.reshape(2, 4, 4, 16)
 
 

time: 95.6 us -> 88.6 us (0.927)
  blocking collectives: 22.5 us -> 51.5 us
  waiting for transfers between devices: 31.6 us -> 10.3 us
  starting transfers between devices: 22.8 us -> 6.94 us
  local copies, waits for them, and re-layouts: 4.16 us -> 2.64 us
  between operations: 1.49 us -> 2.64 us
    all_to_all x1 -> x2, blocking collectives: 22.5 us -> 51.5 us  [the longest x1 29.1 us: elementals(): own = lax.all_to_all(cut, 'vec', 0, 0, axis_index_groups=cores)]
    all_to_all x1 -> x0, waiting for transfers between devices: 12.9 us -> none  [local(): own = lax.all_to_all(cut, 'vec', 0, 0, axis_index_groups=cores)]
    all_to_all x1 -> x0, starting transfers between devices: 10.1 us -> none  [local(): own = lax.all_to_all(cut, 'vec', 0, 0, axis_index_groups=cores)]
    ppermute x4 -> x2, waiting for transfers between devices: 10.6 us -> 1.71 us  [the longest x1 1.71 us: elementals(): other = lax.ppermute(bulk, 'vec', partner)]
    ppermute x4 -> x2, starting transfers between devices: 6.77 us -> 2.73 us  [the longest x1 2.64 us: local(): ahead = lax.ppermute(first_out, 'space', down)]
    ppermute x1, waiting for transfers between devices: 1.17 us -> 4.16 us  [local(): behind = lax.ppermute(w, 'space', up)]
    ppermute x1, waiting for transfers between devices: 6.9 us -> 4.46 us  [local(): behind2 = lax.ppermute(w, 'space', up)]
    ppermute x1, starting transfers between devices: 1.65 us -> 0.01 us  [local(): behind = lax.ppermute(w, 'space', up)]
  transfers between devices with their start and end apart: 8 -> 5, of which waited for: 5 -> 3; matrix products, arithmetic and copies ran while one was open for 5% -> 6% of each run, Pallas kernels for 3% -> 3%
where the time goes in v3:
time: 88.6 us; the launch traced here: 88.2 us
  blocking collectives  51.5 us (58%)
  waiting for transfers between devices  10.3 us (12%)
  Pallas kernels  9.5 us (11%)
  starting transfers between devices  6.94 us (8%)
  other arithmetic  4.64 us (5%)
  local copies, waits for them, and re-layouts  2.64 us (3%)
  between operations  2.64 us (3%)
    all_to_all x1, blocking collectives, elementals(): own = lax.all_to_all(cut, 'vec', 0, 0, axis_index_groups=cores)  29.1 us
    all_to_all x1, blocking collectives, elementals(): lax.all_to_all(sums, ('space', 'vec'), 0, 0, axis_index_groups=alike)  22.4 us
    ppermute x1, waiting for transfers between devices, local(): behind2 = lax.ppermute(w, 'space', up)  4.46 us
    ppermute x1, waiting for transfers between devices, local(): behind = lax.ppermute(w, 'space', up)  4.16 us
    ppermute x1, starting transfers between devices, local(): ahead2 = lax.ppermute(first, 'space', down)  4.12 us
    pallas_call x1, Pallas kernels, elementals(): call(functools.partial(gram_body, scale, along_x, along_y), struct(slabs,...  2.7 us
    ppermute x1, starting transfers between devices, local(): ahead = lax.ppermute(first_out, 'space', down)  2.64 us
    pallas_call x1, Pallas kernels, elementals(): call(functools.partial(second_body, along_y), struct(16, 72 if along_y el...  1.98 us
  transfers between devices with their start and end apart: 5, of which 3 were waited for; matrix products, arithmetic and copies ran while one was open for 6% of the time, Pallas kernels for 3%

profile of v3, /device:TPU:32, one launch (start us, length us, event | category | flops | bytes accessed | tf_op | source)
XLA Modules:
  0.0 88.2 jit_solution(1553127685119820514)
XLA Ops:
  0.0 0.0 copy-start.1
  0.0 0.0 copy-start
  0.0 1.4 %shard_map.51 = f32[808,128]{1,0:T(8,128)S(1)} custom-call(f32[24,32,128]{2,1,0:T(8,128)} %bitcast.42, f32[54,32,128]{2,1,0:T(8,128)} %bitcast.33), custom_call_target="tpu_custom_call" | custom-call | flops 3145728 | bytes 1179648 | tf_op jit(solution)/shard_map/pallas_call | solution.py:387
  1.4 0.0 copy-done.1
  1.4 2.6 %collective-permute-start.8 = (f32[24,32,128]{2,1,0:T(8,128)S(1)}, f32[24,32,128]{2,1,0:T(8,128)S(1)}, u32[]{:S(2)}, u32[]{:S(2)}) collective-permute-start(f32[24,32,128]{2,1,0:T(8,128)S(1)} %bitcast.43), channel_id=1, source_target_pairs={{0,224},{32,0},{64,32},{96,64},{128,96},{160,128},{192,160},{224,1... | collective-permute-start | bytes 1179656 | tf_op jit(solution)/shard_map/ppermute | solution.py:390
  4.0 0.0 collective-permute-start.9
  4.0 0.0 copy-start.3
  4.0 0.7 copy-done.3
  4.7 0.7 fusion.18
  6.6 0.0 copy-done
  6.7 1.1 %shard_map.50.acc_ref = f32[24,32,128]{2,1,0:T(8,128)S(1)} custom-call(f32[24,32,128]{2,1,0:T(8,128)S(1)} %bitcast.44, f32[54,32,128]{2,1,0:T(8,128)S(1)} %bitcast.34), custom_call_target="tpu_custom_call" | custom-call | flops 12582912 | bytes 1966080 | tf_op jit(solution)/shard_map/pallas_call | solution.py:394
  7.7 0.0 copy-start.4
  7.8 0.6 copy-done.4
  8.4 0.6 compare_reduce_fusion
  10.3 0.6 compare_select_fusion.4
  11.0 1.3 %compare_and_fusion = (pred[128]{0:T(512)(128)(4,1)S(1)}, pred[128]{0:T(512)(128)(4,1)S(1)}) fusion(s32[]{:T(128)} %bitcast.20, s32[]{:T(128)} %bitcast.16), kind=kLoop, calls=%fused_computation.13 | loop fusion | flops 3328 | bytes 264 | tf_op jit(solution)/shard_map/jit(remainder)/and | solution.py:411
  12.3 0.7 compare_select_fusion
  13.0 0.0 collective-permute-done.8.ahead_ref
  13.0 4.2 %collective-permute-done.9.behind_ref = f32[808,128]{1,0:T(8,128)S(1)} collective-permute-done((f32[808,128]{1,0:T(8,128)S(1)}, f32[808,128]{1,0:T(8,128)S(1)}, u32[]{:S(2)}, u32[]{:S(2)}) %collective-permute-start.9) | collective-permute-done | bytes 413728 | tf_op jit(solution)/shard_map/ppermute | solution.py:389
  17.2 0.4 shard_map.52
  17.6 0.1 collective-permute-start.11
  17.7 4.1 %collective-permute-start.10 = (f32[24,32,128]{2,1,0:T(8,128)S(1)}, f32[24,32,128]{2,1,0:T(8,128)}, u32[]{:S(2)}, u32[]{:S(2)}) collective-permute-start(f32[24,32,128]{2,1,0:T(8,128)S(1)} %get-tuple-element.117.v_ref), channel_id=1, source_target_pairs={{0,224},{32,0},{64,32},{96,64},{128,96},{160,128},{192,160},{224,1... | collective-permute-start | bytes 1179656 | tf_op jit(solution)/shard_map/ppermute | solution.py:398
  21.8 1.3 %fusion.13 = (f32[1,1,2,128]{3,2,1,0:T(2,128)S(1)}, f32[1,1,2,128]{3,2,1,0:T(2,128)S(1)}) fusion(pred[128]{0:T(512)(128)(4,1)S(1)} %get-tuple-element.141, s32[128]{0:T(128)S(1)} %get-tuple-element.136, s32[128]{0:T(128)S(1)} %get-tuple-element.137, s32[128]{0:T(128)S(1)} %and_select_fusion.4, s32[]{:T(128)} %bitcast.15, f32[]{:T(128)S(6)} %div.34, ...), kind=kLoop, calls=%fused_computation.34 | loop fusion | flops 10496 | bytes 4888 | tf_op jit(solution)/shard_map/stack | solution.py:413
  23.1 0.1 fusion.15
  23.2 0.7 shard_map.54
  23.9 1.1 %shard_map.53 = f32[24,32,128]{2,1,0:T(8,128)S(1)} custom-call(f32[24,32,128]{2,1,0:T(8,128)S(1)} %get-tuple-element.117.v_ref, f32[54,32,128]{2,1,0:T(8,128)S(1)} %bitcast.37), custom_call_target="tpu_custom_call" | custom-call | flops 12582912 | bytes 1966080 | tf_op jit(solution)/shard_map/pallas_call | solution.py:400
  25.0 4.5 %collective-permute-done.11 = f32[24,32,128]{2,1,0:T(8,128)S(1)} collective-permute-done((f32[24,32,128]{2,1,0:T(8,128)S(1)}, f32[24,32,128]{2,1,0:T(8,128)S(1)}, u32[]{:S(2)}, u32[]{:S(2)}) %collective-permute-start.11) | collective-permute-done | bytes 393248 | tf_op jit(solution)/shard_map/ppermute | solution.py:399
  29.5 0.0 collective-permute-done.10
  29.5 58.1 %conditional.1 = (f32[2,4,4,16]{3,2,1,0:T(4,128)S(1)}) conditional(s32[]{:T(128)} %clamp.3, (f32[24,32,128]{2,1,0:T(8,128)S(1)}, f32[24,32,128]{2,1,0:T(8,128)}, f32[24,32,128]{2,1,0:T(8,128)S(1)}, f32[24,32,128]{2,1,0:T(8,128)S(1)}, f32[54,32,128]{2,1,0:T(8,128)S(1)}, /*index=5*/s32[2]{0:T(128)S(1)}, ...), branch_computations={%region_2.3_spmd, %region_3.4_spmd, %region_4.5_spmd, %region_5.6_... | conditional | flops 635437056 | bytes 12320896 | solution.py:450
  29.5 2.0 %branch_2_fun.3 = f32[16,72,128]{2,1,0:T(8,128)S(1)} custom-call(f32[24,32,128]{2,1,0:T(8,128)S(1)} %get-tuple-element.92.acc_ref, f32[24,32,128]{2,1,0:T(8,128)} %get-tuple-element.93.ahead_ref, f32[24,32,128]{2,1,0:T(8,128)S(1)} %get-tuple-element.94.behind_ref, f32[24,32,128]{2,1,0:T(8,128)S(1)} %get-tuple-element.95.v_ref, ...), custom_call_target="tpu_custom_call" | custom-call | flops 6291456 | bytes 2752512 | tf_op jit(solution)/shard_map/cond/branch_2_fun/pallas_call | solution.py:421
  31.5 29.1 %all_to_all.36.own_ref = f32[16,72,128]{2,1,0:T(8,128)S(1)} all-to-all(f32[16,72,128]{2,1,0:T(8,128)S(1)} %branch_2_fun.3), channel_id=1, replica_groups={{0,2,4,6,8,10,12,14,16,18,20,22,24,26,28,30},{1,3,5,7,9,11,13,15,17,19,..., dimensions={0} | all-to-all | bytes 1179648 | tf_op jit(solution)/shard_map/cond/branch_2_fun/all_to_all | solution.py:429
  60.6 0.1 collective-permute-start.4
  60.7 1.7 %collective-permute-done.4.other_ref = f32[16,48,128]{2,1,0:T(8,128)S(1)} collective-permute-done((f32[16,48,128]{2,1,0:T(8,128)S(1)}, f32[16,48,128]{2,1,0:T(8,128)S(1)}, u32[]{:S(2)}, u32[]{:S(2)}) %collective-permute-start.4) | collective-permute-done | bytes 393248 | tf_op jit(solution)/shard_map/cond/branch_2_fun/ppermute | solution.py:435
  62.4 2.7 %branch_2_fun.4 = f32[8,64,128]{2,1,0:T(8,128)S(1)} custom-call(s32[2]{0:T(128)S(1)} %get-tuple-element.91.sc, f32[16,72,128]{2,1,0:T(8,128)S(1)} %all_to_all.36.own_ref, f32[16,48,128]{2,1,0:T(8,128)S(1)} %collective-permute-done.4.other_ref, f32[16,48,128]{2,1,0:T(8,128)S(1)} %slice.30.ahead_ref.behind_ref, f32[16,48,128]{2,1,0:T(8,128)S(1)} %slice.30.ahead_ref.behind_ref, ...), custom_call_target="tpu_custom_call" | custom-call | flops 629145600 | bytes 2359296 | tf_op jit(solution)/shard_map/cond/branch_2_fun/pallas_call | solution.py:436
  65.2 22.4 %all_to_all.37 = f32[128,4,128]{2,1,0:T(4,128)S(1)} all-to-all(f32[128,4,128]{2,1,0:T(4,128)S(1)} %bitcast.31), channel_id=1, replica_groups={{0,2,4,6,8,10,12,14,16,18,20,22,24,26,28,30,32,34,36,38,40,42,44,46,48,..., dimensions={0} | all-to-all | bytes 524288 | tf_op jit(solution)/shard_map/cond/branch_2_fun/all_to_all | solution.py:447
  87.5 0.1 branch_2_fun.5
  87.6 0.0 copy-start.2
  87.6 0.6 copy-done.2
  (4 shorter events, 0.0 us)
Async XLA Ops:
  0.0 1.4 %copy-start.1 = (f32[2,3,4,1,4096]{4,3,2,1,0:T(1,128)S(1)}, f32[2,3,4,1,4096]{4,3,2,1,0:T(1,128)}, u32[]{:S(2)}) copy-start(f32[2,3,4,1,4096]{4,3,2,1,0:T(1,128)} %param.8) | copy-start | bytes 1179652
  0.0 6.6 %copy-start = (f32[3,2,3,3,1,4096]{5,4,3,2,1,0:T(1,128)S(1)}, f32[3,2,3,3,1,4096]{5,4,3,2,1,0:T(1,128)}, u32[]{:S(2)}) copy-start(f32[3,2,3,3,1,4096]{5,4,3,2,1,0:T(1,128)} %param.9) | copy-start | bytes 2654212
  1.4 11.6 %collective-permute-start.8 = (f32[24,32,128]{2,1,0:T(8,128)S(1)}, f32[24,32,128]{2,1,0:T(8,128)S(1)}, u32[]{:S(2)}, u32[]{:S(2)}) collective-permute-start(f32[24,32,128]{2,1,0:T(8,128)S(1)} %bitcast.43), channel_id=1, source_target_pairs={{0,224},{32,0},{64,32},{96,64},{128,96},{160,128},{192,160},{224,1... | collective-permute-start | bytes 1179656 | tf_op jit(solution)/shard_map/ppermute | solution.py:390
  4.0 13.1 %collective-permute-start.9 = (f32[808,128]{1,0:T(8,128)S(1)}, f32[808,128]{1,0:T(8,128)S(1)}, u32[]{:S(2)}, u32[]{:S(2)}) collective-permute-start(f32[808,128]{1,0:T(8,128)S(1)} %shard_map.51), channel_id=1, source_target_pairs={{0,32},{32,64},{64,96},{96,128},{128,160},{160,192},{192,224},{224... | collective-permute-start | bytes 1241096 | tf_op jit(solution)/shard_map/ppermute | solution.py:389
  4.0 0.7 copy-start.3
  7.7 0.7 copy-start.4
  17.6 11.9 %collective-permute-start.11 = (f32[24,32,128]{2,1,0:T(8,128)S(1)}, f32[24,32,128]{2,1,0:T(8,128)S(1)}, u32[]{:S(2)}, u32[]{:S(2)}) collective-permute-start(f32[24,32,128]{2,1,0:T(8,128)S(1)} %get-tuple-element.120), channel_id=1, source_target_pairs={{0,32},{32,64},{64,96},{96,128},{128,160},{160,192},{192,224},{224... | collective-permute-start | bytes 1179656 | tf_op jit(solution)/shard_map/ppermute | solution.py:399
  17.7 11.8 %collective-permute-start.10 = (f32[24,32,128]{2,1,0:T(8,128)S(1)}, f32[24,32,128]{2,1,0:T(8,128)}, u32[]{:S(2)}, u32[]{:S(2)}) collective-permute-start(f32[24,32,128]{2,1,0:T(8,128)S(1)} %get-tuple-element.117.v_ref), channel_id=1, source_target_pairs={{0,224},{32,0},{64,32},{96,64},{128,96},{160,128},{192,160},{224,1... | collective-permute-start | bytes 1179656 | tf_op jit(solution)/shard_map/ppermute | solution.py:398
  60.6 1.8 %collective-permute-start.4 = (f32[16,48,128]{2,1,0:T(8,128)S(1)}, f32[16,48,128]{2,1,0:T(8,128)S(1)}, u32[]{:S(2)}, u32[]{:S(2)}) collective-permute-start(f32[16,48,128]{2,1,0:T(8,128)S(1)} %slice.30.ahead_ref.behind_ref), channel_id=1, source_target_pairs={{0,1},{1,0},{2,3},{3,2},{4,5},{5,4},{6,7},{7,6},{8,9},{9,8},{10,11... | collective-permute-start | bytes 1179656 | tf_op jit(solution)/shard_map/cond/branch_2_fun/ppermute | solution.py:435
  87.6 0.6 copy-start.2

commit v4 on v3

--- a/solution.py
+++ b/solution.py
@@ -14,6 +14,7 @@
 NDISP = 2
 ROWS = 32
 LANES = 128
+PHASES = 36 * NDISP
 VMEM = pltpu.VMEM
 F32 = jnp.float32
 
@@ -21,11 +22,15 @@
 LINKS = pl.BlockSpec((18, ROWS, LANES), lambda i: (0, 0, 0))
 
 
+SMEM_BLOCK = pl.BlockSpec(memory_space=pltpu.SMEM)
+
+
 def call(body, out_shape, ins, scratch=(), flops=0, nbytes=0, room=8):
     kinds = {
-        "s": pl.BlockSpec(memory_space=pltpu.SMEM),
+        "s": SMEM_BLOCK,
         "x": LINKS,
         "v": pl.BlockSpec(memory_space=VMEM),
+        "h": pl.BlockSpec(memory_space=pl.ANY),
     }
     specs = [kinds[letter] for letter in ins]
     many = isinstance(out_shape, (list, tuple))
@@ -34,7 +39,10 @@
         out_shape=out_shape,
         grid=(1,) if "x" in ins else (),
         in_specs=specs,
-        out_specs=[pl.BlockSpec(memory_space=VMEM)] * len(out_shape)
+        out_specs=[
+            pl.BlockSpec(memory_space=VMEM) if each.dtype != jnp.int32 else SMEM_BLOCK
+            for each in out_shape
+        ]
         if many
         else pl.BlockSpec(memory_space=VMEM),
         scratch_shapes=list(scratch),
@@ -105,27 +113,39 @@
     return lambda reim, row, col: g_ref[direction * 18 + reim * 9 + row * 3 + col]
 
 
-def start_body(v_ref, g_ref, w_ref):
+def start_body(v_hbm, g_hbm, va_ref, vb_ref, wa_ref, wb_ref, g_ref, sems):
+    copies = []
+    for i in range(6):
+        for half, v_ref in enumerate((va_ref, vb_ref)):
+            copies.append(
+                pltpu.make_async_copy(
+                    v_hbm.at[pl.ds(4 * i + 2 * half, 2)],
+                    v_ref.at[pl.ds(2 * i, 2)],
+                    sems.at[2 * i + half],
+                )
+            )
+        copies.append(
+            pltpu.make_async_copy(
+                g_hbm.at[pl.ds(3 * i, 3)], g_ref.at[pl.ds(3 * i, 3)], sems.at[12 + i]
+            )
+        )
+    for copy in copies:
+        copy.start()
+    for copy in copies:
+        copy.wait()
     link = plane_link(g_ref, 0)
-
-    def one(n, carry):
-        out = times_dagger(link, [v_ref[4 * k + n] for k in range(6)])
-        for k in range(6):
-            w_ref[pl.ds((4 * k + n) * ROWS, ROWS), :] = out[k]
-        return carry
-
-    lax.fori_loop(0, 4, one, 0)
-    block = lax.axis_index("vec") // 2
-    for n in range(18):
-        w_ref[24 * ROWS + 2 * n : 24 * ROWS + 2 * n + 2, :] = g_ref[n, pl.ds(2 * block, 2), :]
-    w_ref[24 * ROWS + 36 :, :] = jnp.zeros((4, LANES), F32)
+    for v_ref, w_ref in ((va_ref, wa_ref), (vb_ref, wb_ref)):
+        for n in range(2):
+            out = times_dagger(link, [v_ref[2 * k + n] for k in range(6)])
+            for k in range(6):
+                w_ref[(2 * k + n) * ROWS : (2 * k + n + 1) * ROWS, :] = out[k]
 
 
 def inner_body(v_ref, g_ref, acc_ref):
     link_y, link_z = plane_link(g_ref, 1), plane_link(g_ref, 2)
 
     def one(n, carry):
-        field = [v_ref[4 * k + n] for k in range(6)]
+        field = [v_ref[2 * k + n] for k in range(6)]
         total = times(link_y, [y_next(x) for x in field])
         for part in (
             [y_prev(x) for x in times_dagger(link_y, field)],
@@ -134,44 +154,61 @@
         ):
             total = [a + b for a, b in zip(total, part)]
         for k in range(6):
-            acc_ref[4 * k + n] = total[k]
+            acc_ref[2 * k + n] = total[k]
         return carry
 
-    lax.fori_loop(0, 4, one, 0)
-
-
-def first_body(acc_ref, ahead_ref, behind_ref, g_ref, first_ref, w_ref):
+    lax.fori_loop(0, 2, one, 0)
+
+
+def summed(n, acc_ref, ahead_ref, behind_ref, link):
+    hop = times(link, [ahead_ref[2 * k + n] for k in range(6)])
+    return [
+        acc_ref[2 * k + n] + hop[k] + behind_ref[pl.ds((2 * k + n) * ROWS, ROWS), :]
+        for k in range(6)
+    ]
+
+
+def first_body(links_too, acc_ref, ahead_ref, behind_ref, g_ref, first_ref, w_ref):
     link = plane_link(g_ref, 0)
 
     def one(n, carry):
-        hop = times(link, [ahead_ref[4 * k + n] for k in range(6)])
-        first = [
-            (acc_ref[4 * k + n] + hop[k] + behind_ref[pl.ds((4 * k + n) * ROWS, ROWS), :]) / -6.0
-            for k in range(6)
-        ]
+        first = [x / -6.0 for x in summed(n, acc_ref, ahead_ref, behind_ref, link)]
         out = times_dagger(link, first)
         for k in range(6):
-            first_ref[4 * k + n] = first[k]
-            w_ref[4 * k + n] = out[k]
+            first_ref[2 * k + n] = first[k]
+            w_ref[pl.ds((2 * k + n) * ROWS, ROWS), :] = out[k]
         return carry
 
-    lax.fori_loop(0, 4, one, 0)
-
-
-def second_body(edges, acc_ref, ahead_ref, behind_ref, v_ref, g_ref, out_ref, f_ref, half_ref):
+    lax.fori_loop(0, 2, one, 0)
+    if links_too:
+        block = lax.axis_index("vec") // 2
+        for n in range(18):
+            at = 12 * ROWS + 2 * n
+            w_ref[at : at + 2, :] = g_ref[n, pl.ds(2 * block, 2), :]
+        w_ref[12 * ROWS + 36 :, :] = jnp.zeros((4, LANES), F32)
+
+
+def filter_half(half, acc_ref, ahead_ref, behind_ref, v_ref, link, f_ref, half_ref):
+    def one(n, carry):
+        total = summed(n, acc_ref, ahead_ref, behind_ref, link)
+        for k in range(6):
+            f = total[k] / -3.0 - v_ref[2 * k + n]
+            at = pl.ds((4 * k + 2 * half + n) * ROWS, ROWS)
+            f_ref[at, :] = f
+            if half_ref is not None:
+                half_ref[at, :] = pltpu.roll(f, NZ, 1)
+        return carry
+
+    lax.fori_loop(0, 2, one, 0)
+
+
+def second_body(
+    edges, acca, aheada, behinda, va, accb, aheadb, behindb, vb, g_ref, out_ref, f_ref, half_ref
+):
     link = plane_link(g_ref, 0)
-
-    def one(n, carry):
-        hop = times(link, [ahead_ref[4 * k + n] for k in range(6)])
-        for k in range(6):
-            r = 4 * k + n
-            f = (acc_ref[r] + hop[k] + behind_ref[r]) / -3.0 - v_ref[r]
-            f_ref[pl.ds(r * ROWS, ROWS), :] = f
-            if edges:
-                half_ref[pl.ds(r * ROWS, ROWS), :] = pltpu.roll(f, NZ, 1)
-        return carry
-
-    lax.fori_loop(0, 4, one, 0)
+    rolled = half_ref if edges else None
+    filter_half(0, acca, aheada, behinda, va, link, f_ref, rolled)
+    filter_half(1, accb, aheadb, behindb, vb, link, f_ref, rolled)
     low = lane_of((24, LANES)) < NZ
     for block in range(16):
         for q in range(2):
@@ -183,7 +220,23 @@
         out_ref[block, 48:72, :] = jnp.where(low, under, over)
 
 
-def matrix_body(sc, g_ref, behind_ref, m_ref):
+def table_body(slabs, sc, mom, g_ref, behind_ref, m_ref, case_ref):
+    first, second = lax.rem(sc[0], 3), lax.rem(sc[1], 3)
+    along_x = (first == 0) | (second == 0)
+    along_y = (first == 1) | (second == 1)
+    case_ref[0] = along_x.astype(jnp.int32) + 2 * along_y.astype(jnp.int32)
+    here = 4 * (lax.axis_index("vec") // 2)
+    lane = lane_of((1, LANES))
+    for op in range(NMOM):
+        part_x = ((mom[op, 0] * lax.axis_index("space")) & (slabs - 1)).astype(F32) / slabs
+        part_z = ((mom[op, 2] * (lane & (NZ - 1))) & (NZ - 1)).astype(F32) / NZ
+        for q in range(2):
+            row = here + 2 * q + lane // NZ
+            part_y = ((mom[op, 1] * row) & (NY - 1)).astype(F32) / NY
+            angle = (part_x + part_y + part_z) * (2.0 * math.pi)
+            at = PHASES + 4 * op + q
+            m_ref[at : at + 1, :] = jnp.cos(angle)
+            m_ref[at + 2 : at + 3, :] = jnp.sin(angle)
     block = lax.axis_index("vec") // 2
     low = lane_of((1, LANES)) < NZ
     for op in range(NDISP):
@@ -212,7 +265,7 @@
 
         @pl.when(hop == 3)
         def _():
-            dagger(lambda n, q: behind_ref[24 * ROWS + 2 * n + q : 24 * ROWS + 2 * n + q + 1, :])
+            dagger(lambda n, q: behind_ref[12 * ROWS + 2 * n + q : 12 * ROWS + 2 * n + q + 1, :])
 
         @pl.when(hop == 4)
         def _():
@@ -245,7 +298,8 @@
 
 
 def gram_body(
-    scale, along_x, along_y, sc, own_ref, other_ref, ahead_ref, behind_ref, m_ref, ph_ref, out_ref,
+    scale, along_x, along_y, sc, own_ref, other_ref, ahead_ref, behind_ref, m_ref,
+    out_ref,
     f_ref, n_ref, lhs_hi, lhs_lo, rhs_hi, rhs_lo,
 ):
     core = lax.rem(lax.axis_index("vec"), 2)
@@ -280,8 +334,8 @@
                 f_ref[2 * pair + odd_one, q] = rows_of_block(own_ref, tile, odd_one)
     for q in range(2):
         for op in range(NMOM):
-            cosine = ph_ref[4 * op + q : 4 * op + q + 1, :]
-            sine = ph_ref[4 * op + 2 + q : 4 * op + 3 + q, :]
+            at = PHASES + 4 * op + q
+            cosine, sine = m_ref[at : at + 1, :], m_ref[at + 2 : at + 3, :]
             for c in range(3):
                 re, im = f_ref[c, q], f_ref[3 + c, q]
                 put_lhs(op, c, q, cosine * re + sine * im)
@@ -375,57 +429,58 @@
     field_bytes = 24 * ROWS * LANES * 4
     field = vectors.reshape(24, ROWS, LANES)
     gauge = gauge_links.reshape(54, ROWS, LANES)
-    slab = lax.axis_index("space")
-    block = lax.axis_index("vec") // 2
     up = [(i, (i + 1) % slabs) for i in range(slabs)]
     down = [(i, (i - 1) % slabs) for i in range(slabs)]
     partner = [(i, i ^ 1) for i in range(vecs)]
     cores = [[2 * i + c for i in range(vecs // 2)] for c in range(2)]
     alike = [[2 * i + c for i in range(slabs * vecs // 2)] for c in range(2)]
 
-    shape = struct(24 * ROWS + 40, LANES)
-    w = call(start_body, shape, "vx", flops=3 << 20, nbytes=3 * field_bytes)(field, gauge)
-    first_out, w = lax.optimization_barrier((field, w))
-    behind = lax.ppermute(w, "space", up)
-    ahead = lax.ppermute(first_out, "space", down)
-    inner = call(
-        inner_body, struct(24, ROWS, LANES), "vv", flops=12 << 20, nbytes=5 * field_bytes
-    )
-    acc = inner(field, gauge)
-    first, w = call(
-        first_body, [struct(24, ROWS, LANES)] * 2, "vvvx", flops=6 << 20, nbytes=6 * field_bytes
-    )(acc, ahead, behind, gauge)
-    ahead2 = lax.ppermute(first, "space", down)
-    behind2 = lax.ppermute(w, "space", up)
-    acc = inner(first, gauge)
-    matrices = call(
-        matrix_body, struct(72, LANES), "svv", flops=1 << 20, nbytes=4 * field_bytes
-    )(displacements, gauge, behind)
-    lane = jnp.arange(LANES, dtype=jnp.int32)
-    row = 4 * block + 2 * jnp.arange(2, dtype=jnp.int32)[:, None] + lane[None, :] // NZ
-    depth = jnp.broadcast_to(lane % NZ, row.shape)
-    angles = []
-    for op in range(NMOM):
-        part_x = (momenta[op, 0] * slab % slabs).astype(F32) / slabs
-        part_y = (momenta[op, 1] * row % NY).astype(F32) / NY
-        part_z = (momenta[op, 2] * depth % NZ).astype(F32) / NZ
-        angles.append((part_x + part_y + part_z) * (2.0 * math.pi))
-    angle = jnp.stack(angles)
-    phases = jnp.stack([jnp.cos(angle), jnp.sin(angle)], axis=1).reshape(8, LANES)
-    along = displacements % 3
-    case = jnp.any(along == 0).astype(jnp.int32) + 2 * jnp.any(along == 1).astype(jnp.int32)
-    acc, phases, matrices, case = lax.optimization_barrier((acc, phases, matrices, case))
+    half = struct(12, ROWS, LANES)
+    rows = struct(12 * ROWS, LANES)
+    va, vb, wa, wb = call(
+        start_body,
+        [half, half, rows, rows],
+        "hh",
+        scratch=[VMEM((18, ROWS, LANES), F32), pltpu.SemaphoreType.DMA((18,))],
+        flops=3 << 20,
+        nbytes=3 * field_bytes,
+    )(field, gauge)
+    inner = call(inner_body, half, "vv", flops=6 << 20, nbytes=3 * field_bytes)
+
+    def step(links_too, *operands):
+        w = struct(12 * ROWS + 40, LANES) if links_too else rows
+        body = functools.partial(first_body, links_too)
+        return call(body, [half, w], "vvvx", flops=3 << 20, nbytes=3 * field_bytes)(*operands)
+
+    def exchange(v, w):
+        return lax.ppermute(v, "space", down), lax.ppermute(w, "space", up)
+
+    aheada, behinda = exchange(va, wa)
+    aheadb, behindb = exchange(vb, wb)
+    firsta, wa = step(True, inner(va, gauge), aheada, behinda, gauge)
+    ahead2a, behind2a = exchange(firsta, wa)
+    firstb, wb = step(False, inner(vb, gauge), aheadb, behindb, gauge)
+    ahead2b, behind2b = exchange(firstb, wb)
+    acca, accb = inner(firsta, gauge), inner(firstb, gauge)
+    table, case = call(
+        functools.partial(table_body, slabs),
+        [struct(PHASES + 4 * NMOM, LANES), jax.ShapeDtypeStruct((1,), jnp.int32)],
+        "ssvv",
+        flops=1 << 20,
+        nbytes=4 * field_bytes,
+    )(displacements, momenta, gauge, behind2a)
+    acca, accb, table, case = lax.optimization_barrier((acca, accb, table, case))
     scale = 1.0 / math.sqrt(3 * slabs * NY * NZ)
 
-    def elementals(along_x, along_y, acc, ahead2, behind2, field, gauge, phases, matrices):
+    def elementals(along_x, along_y, fields, gauge, table):
         cut = call(
             functools.partial(second_body, along_y),
             struct(16, 72 if along_y else 48, LANES),
-            "vvvvx",
+            "vvvvvvvvx",
             scratch=[VMEM((24 * ROWS, LANES), F32)] * 2,
             flops=6 << 20,
             nbytes=7 * field_bytes,
-        )(acc, ahead2, behind2, field, gauge)
+        )(*fields, gauge)
         own = lax.all_to_all(cut, "vec", 0, 0, axis_index_groups=cores)
         bulk = own[:, :48]
         ahead3 = behind3 = bulk
@@ -436,24 +491,26 @@
         sums = call(
             functools.partial(gram_body, scale, along_x, along_y),
             struct(slabs, 64, LANES),
-            "svvvvvv",
+            "svvvvv",
             scratch=[VMEM((6, 2, 64, LANES), F32)] * 2
             + [VMEM((256, 12 * LANES), jnp.bfloat16)] * 4,
             room=16,
             flops=600 << 20,
             nbytes=6 * field_bytes,
-        )(displacements, own, other, ahead3, behind3, matrices, phases)
+        )(displacements, own, other, ahead3, behind3, table)
         sums = sums.reshape(slabs * vecs // 2, 4, LANES)
         parts = lax.all_to_all(sums, ("space", "vec"), 0, 0, axis_index_groups=alike)
         return call(finish_body, struct(8, 4, 16), "v")(parts.reshape(512, LANES))
 
     out = lax.switch(
-        case,
+        case[0],
         [
             functools.partial(elementals, bool(i & 1), bool(i & 2))
             for i in range(4)
         ],
-        acc, ahead2, behind2, field, gauge, phases, matrices,
+        (acca, ahead2a, behind2a, va, accb, ahead2b, behind2b, vb),
+        gauge,
+        table,
     )
     return out.reshape(2, 4, 4, 16)
 

time: 88.6 us -> 83.9 us (0.947); the launches traced: 88.2 us -> 85 us
  starting transfers between devices: 6.94 us -> 22.4 us
  blocking collectives: 51.5 us -> 44.4 us
  other arithmetic: 4.64 us -> 0 us
  waiting for transfers between devices: 10.3 us -> 6.9 us
  between operations: 2.64 us -> 0.77 us
  local copies, waits for them, and re-layouts: 2.64 us -> 1.73 us
    ppermute x4 -> x10, starting transfers between devices: 6.84 us -> 22.4 us  [the longest x8 16.9 us: exchange(): return (lax.ppermute(v, 'space', down), lax.ppermute(w, 'space', up))]
    all_to_all x1, blocking collectives: 29.1 us -> 23.7 us  [elementals(): own = lax.all_to_all(cut, 'vec', 0, 0, axis_index_groups=cores)]
    ppermute x4 -> x10, waiting for transfers between devices: 8.62 us -> 6.89 us  [the longest x1 5.75 us: elementals(): behind3 = lax.ppermute(bulk, 'space', up)]
    ppermute x1, waiting for transfers between devices: 1.71 us -> 0.01 us  [elementals(): other = lax.ppermute(bulk, 'vec', partner)]
    all_to_all x1, blocking collectives: 22.4 us -> 20.7 us  [elementals(): lax.all_to_all(sums, ('space', 'vec'), 0, 0, axis_index_groups=alike)]
    pallas_call x1, Pallas kernels: 1.98 us -> 0.51 us  [elementals(): call(functools.partial(second_body, along_y), struct(16, 72 if along_y el...]
    rem x2 -> x0, other arithmetic: 1.33 us -> none  [local(): part_z = (momenta[op, 2] * depth % NZ).astype(F32) / NZ]
    and x1 -> x0, other arithmetic: 1.32 us -> none  [local(): part_z = (momenta[op, 2] * depth % NZ).astype(F32) / NZ]
  transfers between devices with their start and end apart: 5 -> 11, of which waited for: 3 -> 4; matrix products, arithmetic and copies ran while one was open for 6% -> 0% of each run, Pallas kernels for 3% -> 4%
where the time goes in v4:
time: 83.9 us; the launch traced here: 85 us
  blocking collectives  44.4 us (53%)
  starting transfers between devices  22.4 us (27%)
  Pallas kernels  8.69 us (10%)
  waiting for transfers between devices  6.9 us (8%)
  local copies, waits for them, and re-layouts  1.73 us (2%)
    all_to_all x1, blocking collectives, elementals(): own = lax.all_to_all(cut, 'vec', 0, 0, axis_index_groups=cores)  23.7 us
    all_to_all x1, blocking collectives, elementals(): lax.all_to_all(sums, ('space', 'vec'), 0, 0, axis_index_groups=alike)  20.7 us
    ppermute x8, starting transfers between devices, exchange(): return (lax.ppermute(v, 'space', down), lax.ppermute(w, 'space', up))  16.9 us
    ppermute x1, waiting for transfers between devices, elementals(): behind3 = lax.ppermute(bulk, 'space', up)  5.75 us
    ppermute x1, starting transfers between devices, elementals(): ahead3 = lax.ppermute(bulk, 'space', down)  3.78 us
    pallas_call x1, Pallas kernels, elementals(): call(functools.partial(gram_body, scale, along_x, along_y), struct(slabs,...  2.66 us
    ppermute x1, starting transfers between devices, elementals(): behind3 = lax.ppermute(bulk, 'space', up)  1.77 us
    unnamed x10, local copies, waits for them, and re-layouts  1.73 us
  transfers between devices with their start and end apart: 11, of which 4 were waited for; matrix products, arithmetic and copies ran while one was open for 0% of the time, Pallas kernels for 4%

profile of v4, /device:TPU:32, one launch (start us, length us, event | category | flops | bytes accessed | tf_op | source)
XLA Modules:
  0.0 85.0 jit_solution(15618381484773400303)
XLA Ops:
  0.0 0.0 copy-start
  0.0 1.0 %copy-done = f32[2,3,4,1,4096]{4,3,2,1,0:T(1,128)S(1)} copy-done((f32[2,3,4,1,4096]{4,3,2,1,0:T(1,128)S(1)}, f32[2,3,4,1,4096]{4,3,2,1,0:T(1,128)}, u32[]{:S(2)}) %copy-start) | copy-done | bytes 393240
  1.0 0.0 copy-start.2
  1.0 1.6 %shard_map.50 = (f32[12,32,128]{2,1,0:T(8,128)S(1)}, f32[12,32,128]{2,1,0:T(8,128)S(1)}, f32[384,128]{1,0:T(8,128)S(1)}, f32[384,128]{1,0:T(8,128)S(1)}) custom-call(f32[24,32,128]{2,1,0:T(8,128)S(1)} %bitcast.19, f32[54,32,128]{2,1,0:T(8,128)} %bitcast.24), custom_call_target="tpu_custom_call" | custom-call | flops 3145728 | bytes 1179648 | tf_op jit(solution)/shard_map/pallas_call | solution.py:440
  2.7 1.7 %collective-permute-start.9 = (f32[384,128]{1,0:T(8,128)S(1)}, f32[384,128]{1,0:T(8,128)S(1)}, u32[]{:S(2)}, u32[]{:S(2)}) collective-permute-start(f32[384,128]{1,0:T(8,128)S(1)} %get-tuple-element.158), channel_id=1, source_target_pairs={{0,32},{32,64},{64,96},{96,128},{128,160},{160,192},{192,224},{224... | collective-permute-start | bytes 589832 | tf_op jit(solution)/shard_map/ppermute | solution.py:456
  4.3 2.6 %collective-permute-start.8 = (f32[12,32,128]{2,1,0:T(8,128)S(1)}, f32[12,32,128]{2,1,0:T(8,128)S(1)}, u32[]{:S(2)}, u32[]{:S(2)}) collective-permute-start(f32[12,32,128]{2,1,0:T(8,128)S(1)} %get-tuple-element.157.v_ref), channel_id=1, source_target_pairs={{0,224},{32,0},{64,32},{96,64},{128,96},{160,128},{192,160},{224,1... | collective-permute-start | bytes 589832 | tf_op jit(solution)/shard_map/ppermute | solution.py:456
  6.9 0.0 collective-permute-start.11
  6.9 4.1 %collective-permute-start.10 = (f32[12,32,128]{2,1,0:T(8,128)S(1)}, f32[12,32,128]{2,1,0:T(8,128)S(1)}, u32[]{:S(2)}, u32[]{:S(2)}) collective-permute-start(f32[12,32,128]{2,1,0:T(8,128)S(1)} %get-tuple-element.160.v_ref), channel_id=1, source_target_pairs={{0,224},{32,0},{64,32},{96,64},{128,96},{160,128},{192,160},{224,1... | collective-permute-start | bytes 589832 | tf_op jit(solution)/shard_map/ppermute | solution.py:456
  11.0 0.0 copy-done.2
  11.0 0.5 shard_map.51.acc_ref
  11.5 0.5 collective-permute-done.9.behind_ref
  12.1 0.1 collective-permute-done.8.ahead_ref
  12.1 0.2 shard_map.52
  12.4 1.7 %collective-permute-start.12 = (f32[424,128]{1,0:T(8,128)S(1)}, f32[424,128]{1,0:T(8,128)S(1)}, u32[]{:S(2)}, u32[]{:S(2)}) collective-permute-start(f32[424,128]{1,0:T(8,128)S(1)} %get-tuple-element.163), channel_id=1, source_target_pairs={{0,32},{32,64},{64,96},{96,128},{128,160},{160,192},{192,224},{224... | collective-permute-start | bytes 651272 | tf_op jit(solution)/shard_map/ppermute | solution.py:456
  14.0 0.5 shard_map.54.acc_ref
  14.6 2.6 %collective-permute-start.13 = (f32[12,32,128]{2,1,0:T(8,128)S(1)}, f32[12,32,128]{2,1,0:T(8,128)S(1)}, u32[]{:S(2)}, u32[]{:S(2)}) collective-permute-start(f32[12,32,128]{2,1,0:T(8,128)S(1)} %get-tuple-element.159.v_ref), channel_id=1, source_target_pairs={{0,224},{32,0},{64,32},{96,64},{128,96},{160,128},{192,160},{224,1... | collective-permute-start | bytes 589832 | tf_op jit(solution)/shard_map/ppermute | solution.py:456
  17.2 0.0 collective-permute-done.11.behind_ref
  17.2 0.0 collective-permute-done.10.ahead_ref
  17.2 0.2 shard_map.55
  17.4 0.3 collective-permute-start.15
  17.7 3.9 %collective-permute-start.14 = (f32[12,32,128]{2,1,0:T(8,128)S(1)}, f32[12,32,128]{2,1,0:T(8,128)S(1)}, u32[]{:S(2)}, u32[]{:S(2)}) collective-permute-start(f32[12,32,128]{2,1,0:T(8,128)S(1)} %get-tuple-element.162.v_ref), channel_id=1, source_target_pairs={{0,224},{32,0},{64,32},{96,64},{128,96},{160,128},{192,160},{224,1... | collective-permute-start | bytes 589832 | tf_op jit(solution)/shard_map/ppermute | solution.py:456
  21.6 0.5 shard_map.53
  22.2 0.0 copy-start.1
  22.2 0.0 copy-start.4
  22.2 0.5 shard_map.56
  22.7 0.0 collective-permute-done.12.behind_ref
  22.7 0.1 copy-done.1
  22.9 0.0 copy-done.4
  22.9 1.2 %shard_map.57 = (f32[80,128]{1,0:T(8,128)S(1)}, s32[1]{0:T(128)}) custom-call(s32[2]{0:T(128)S(1)} %copy-done.4, s32[2,3]{1,0:T(2,128)S(1)} %copy-done.1, f32[54,32,128]{2,1,0:T(8,128)S(1)} %bitcast.31, f32[424,128]{1,0:T(8,128)S(1)} %collective-permute-done.12.behind_ref), custom_call_target="tpu_custom_call" | custom-call | flops 1048576 | bytes 1572864 | tf_op jit(solution)/shard_map/pallas_call | solution.py:465
  24.7 0.0 collective-permute-done.13
  24.8 0.5 collective-permute-done.15
  25.3 0.0 collective-permute-done.14
  25.3 59.1 %conditional.1 = (f32[2,4,4,16]{3,2,1,0:T(4,128)S(1)}) conditional(s32[]{:T(128)} %bitcast.14, (f32[12,32,128]{2,1,0:T(8,128)S(1)}, f32[12,32,128]{2,1,0:T(8,128)S(1)}, f32[424,128]{1,0:T(8,128)S(1)}, f32[12,32,128]{2,1,0:T(8,128)S(1)}, f32[12,32,128]{2,1,0:T(8,128)S(1)}, /*index=5*/f32[12,32,128]{2,1,0:T(8,128)S(1)}, ...), branch_computations={%region_0.0_spmd, %region_1.0_spmd, %region_2.0_spmd, %region_3.0_... | conditional | flops 635437056 | bytes 12320896 | solution.py:505
  25.3 0.5 branch_1_fun.3
  25.8 23.7 %all_to_all.34.own_ref = f32[16,48,128]{2,1,0:T(8,128)S(1)} all-to-all(f32[16,48,128]{2,1,0:T(8,128)S(1)} %branch_1_fun.3), channel_id=1, replica_groups={{0,2,4,6,8,10,12,14,16,18,20,22,24,26,28,30},{1,3,5,7,9,11,13,15,17,19,..., dimensions={0} | all-to-all | bytes 786432 | tf_op jit(solution)/shard_map/cond/branch_1_fun/all_to_all | solution.py:484
  49.5 1.8 %collective-permute-start.3 = (f32[16,48,128]{2,1,0:T(8,128)S(1)}, f32[16,48,128]{2,1,0:T(8,128)S(1)}, u32[]{:S(2)}, u32[]{:S(2)}) collective-permute-start(f32[16,48,128]{2,1,0:T(8,128)S(1)} %all_to_all.34.own_ref), channel_id=1, source_target_pairs={{0,32},{32,64},{64,96},{96,128},{128,160},{160,192},{192,224},{224... | collective-permute-start | bytes 1179656 | tf_op jit(solution)/shard_map/cond/branch_1_fun/ppermute | solution.py:489
  51.2 3.8 %collective-permute-start.2 = (f32[16,48,128]{2,1,0:T(8,128)S(1)}, f32[16,48,128]{2,1,0:T(8,128)S(1)}, u32[]{:S(2)}, u32[]{:S(2)}) collective-permute-start(f32[16,48,128]{2,1,0:T(8,128)S(1)} %all_to_all.34.own_ref), channel_id=1, source_target_pairs={{0,224},{32,0},{64,32},{96,64},{128,96},{160,128},{192,160},{224,1... | collective-permute-start | bytes 1179656 | tf_op jit(solution)/shard_map/cond/branch_1_fun/ppermute | solution.py:488
  55.0 0.0 collective-permute-start.1
  55.0 5.7 %collective-permute-done.3.behind_ref = f32[16,48,128]{2,1,0:T(8,128)S(1)} collective-permute-done((f32[16,48,128]{2,1,0:T(8,128)S(1)}, f32[16,48,128]{2,1,0:T(8,128)S(1)}, u32[]{:S(2)}, u32[]{:S(2)}) %collective-permute-start.3) | collective-permute-done | bytes 393248 | tf_op jit(solution)/shard_map/cond/branch_1_fun/ppermute | solution.py:489
  60.8 0.0 collective-permute-done.2.ahead_ref
  60.8 0.0 collective-permute-done.1.other_ref
  60.8 2.7 %branch_1_fun.4 = f32[8,64,128]{2,1,0:T(8,128)S(1)} custom-call(s32[2]{0:T(128)S(1)} %get-tuple-element.110.sc, f32[16,48,128]{2,1,0:T(8,128)S(1)} %all_to_all.34.own_ref, f32[16,48,128]{2,1,0:T(8,128)S(1)} %collective-permute-done.1.other_ref, f32[16,48,128]{2,1,0:T(8,128)S(1)} %collective-permute-done.2.ahead_ref, ...), custom_call_target="tpu_custom_call" | custom-call | flops 629145600 | bytes 2359296 | tf_op jit(solution)/shard_map/cond/branch_1_fun/pallas_call | solution.py:491
  63.5 20.7 %all_to_all.35 = f32[128,4,128]{2,1,0:T(4,128)S(1)} all-to-all(f32[128,4,128]{2,1,0:T(4,128)S(1)} %bitcast.20), channel_id=1, replica_groups={{0,2,4,6,8,10,12,14,16,18,20,22,24,26,28,30,32,34,36,38,40,42,44,46,48,..., dimensions={0} | all-to-all | bytes 524288 | tf_op jit(solution)/shard_map/cond/branch_1_fun/all_to_all | solution.py:502
  84.1 0.1 branch_1_fun.5
  84.4 0.0 copy-start.3
  84.4 0.6 copy-done.3
Async XLA Ops:
  0.0 1.0 %copy-start = (f32[2,3,4,1,4096]{4,3,2,1,0:T(1,128)S(1)}, f32[2,3,4,1,4096]{4,3,2,1,0:T(1,128)}, u32[]{:S(2)}) copy-start(f32[2,3,4,1,4096]{4,3,2,1,0:T(1,128)} %param.8) | copy-start | bytes 1179652
  1.0 10.0 %copy-start.2 = (f32[3,2,3,3,1,4096]{5,4,3,2,1,0:T(1,128)S(1)}, f32[3,2,3,3,1,4096]{5,4,3,2,1,0:T(1,128)}, u32[]{:S(2)}) copy-start(f32[3,2,3,3,1,4096]{5,4,3,2,1,0:T(1,128)} %param.9) | copy-start | bytes 2654212
  2.7 9.4 %collective-permute-start.9 = (f32[384,128]{1,0:T(8,128)S(1)}, f32[384,128]{1,0:T(8,128)S(1)}, u32[]{:S(2)}, u32[]{:S(2)}) collective-permute-start(f32[384,128]{1,0:T(8,128)S(1)} %get-tuple-element.158), channel_id=1, source_target_pairs={{0,32},{32,64},{64,96},{96,128},{128,160},{160,192},{192,224},{224... | collective-permute-start | bytes 589832 | tf_op jit(solution)/shard_map/ppermute | solution.py:456
  4.3 7.8 %collective-permute-start.8 = (f32[12,32,128]{2,1,0:T(8,128)S(1)}, f32[12,32,128]{2,1,0:T(8,128)S(1)}, u32[]{:S(2)}, u32[]{:S(2)}) collective-permute-start(f32[12,32,128]{2,1,0:T(8,128)S(1)} %get-tuple-element.157.v_ref), channel_id=1, source_target_pairs={{0,224},{32,0},{64,32},{96,64},{128,96},{160,128},{192,160},{224,1... | collective-permute-start | bytes 589832 | tf_op jit(solution)/shard_map/ppermute | solution.py:456
  6.9 10.3 %collective-permute-start.11 = (f32[384,128]{1,0:T(8,128)S(1)}, f32[384,128]{1,0:T(8,128)S(1)}, u32[]{:S(2)}, u32[]{:S(2)}) collective-permute-start(f32[384,128]{1,0:T(8,128)S(1)} %get-tuple-element.161), channel_id=1, source_target_pairs={{0,32},{32,64},{64,96},{96,128},{128,160},{160,192},{192,224},{224... | collective-permute-start | bytes 589832 | tf_op jit(solution)/shard_map/ppermute | solution.py:456
  6.9 10.3 %collective-permute-start.10 = (f32[12,32,128]{2,1,0:T(8,128)S(1)}, f32[12,32,128]{2,1,0:T(8,128)S(1)}, u32[]{:S(2)}, u32[]{:S(2)}) collective-permute-start(f32[12,32,128]{2,1,0:T(8,128)S(1)} %get-tuple-element.160.v_ref), channel_id=1, source_target_pairs={{0,224},{32,0},{64,32},{96,64},{128,96},{160,128},{192,160},{224,1... | collective-permute-start | bytes 589832 | tf_op jit(solution)/shard_map/ppermute | solution.py:456
  12.4 10.3 %collective-permute-start.12 = (f32[424,128]{1,0:T(8,128)S(1)}, f32[424,128]{1,0:T(8,128)S(1)}, u32[]{:S(2)}, u32[]{:S(2)}) collective-permute-start(f32[424,128]{1,0:T(8,128)S(1)} %get-tuple-element.163), channel_id=1, source_target_pairs={{0,32},{32,64},{64,96},{96,128},{128,160},{160,192},{192,224},{224... | collective-permute-start | bytes 651272 | tf_op jit(solution)/shard_map/ppermute | solution.py:456
  14.6 10.2 %collective-permute-start.13 = (f32[12,32,128]{2,1,0:T(8,128)S(1)}, f32[12,32,128]{2,1,0:T(8,128)S(1)}, u32[]{:S(2)}, u32[]{:S(2)}) collective-permute-start(f32[12,32,128]{2,1,0:T(8,128)S(1)} %get-tuple-element.159.v_ref), channel_id=1, source_target_pairs={{0,224},{32,0},{64,32},{96,64},{128,96},{160,128},{192,160},{224,1... | collective-permute-start | bytes 589832 | tf_op jit(solution)/shard_map/ppermute | solution.py:456
  17.4 7.9 %collective-permute-start.15 = (f32[384,128]{1,0:T(8,128)S(1)}, f32[384,128]{1,0:T(8,128)S(1)}, u32[]{:S(2)}, u32[]{:S(2)}) collective-permute-start(f32[384,128]{1,0:T(8,128)S(1)} %get-tuple-element.169), channel_id=1, source_target_pairs={{0,32},{32,64},{64,96},{96,128},{128,160},{160,192},{192,224},{224... | collective-permute-start | bytes 589832 | tf_op jit(solution)/shard_map/ppermute | solution.py:456
  17.7 7.6 %collective-permute-start.14 = (f32[12,32,128]{2,1,0:T(8,128)S(1)}, f32[12,32,128]{2,1,0:T(8,128)S(1)}, u32[]{:S(2)}, u32[]{:S(2)}) collective-permute-start(f32[12,32,128]{2,1,0:T(8,128)S(1)} %get-tuple-element.162.v_ref), channel_id=1, source_target_pairs={{0,224},{32,0},{64,32},{96,64},{128,96},{160,128},{192,160},{224,1... | collective-permute-start | bytes 589832 | tf_op jit(solution)/shard_map/ppermute | solution.py:456
  22.2 0.7 copy-start.1
  22.2 0.7 copy-start.4
  49.5 11.3 %collective-permute-start.3 = (f32[16,48,128]{2,1,0:T(8,128)S(1)}, f32[16,48,128]{2,1,0:T(8,128)S(1)}, u32[]{:S(2)}, u32[]{:S(2)}) collective-permute-start(f32[16,48,128]{2,1,0:T(8,128)S(1)} %all_to_all.34.own_ref), channel_id=1, source_target_pairs={{0,32},{32,64},{64,96},{96,128},{128,160},{160,192},{192,224},{224... | collective-permute-start | bytes 1179656 | tf_op jit(solution)/shard_map/cond/branch_1_fun/ppermute | solution.py:489
  51.2 9.5 %collective-permute-start.2 = (f32[16,48,128]{2,1,0:T(8,128)S(1)}, f32[16,48,128]{2,1,0:T(8,128)S(1)}, u32[]{:S(2)}, u32[]{:S(2)}) collective-permute-start(f32[16,48,128]{2,1,0:T(8,128)S(1)} %all_to_all.34.own_ref), channel_id=1, source_target_pairs={{0,224},{32,0},{64,32},{96,64},{128,96},{160,128},{192,160},{224,1... | collective-permute-start | bytes 1179656 | tf_op jit(solution)/shard_map/cond/branch_1_fun/ppermute | solution.py:488
  55.0 5.8 %collective-permute-start.1 = (f32[16,48,128]{2,1,0:T(8,128)S(1)}, f32[16,48,128]{2,1,0:T(8,128)S(1)}, u32[]{:S(2)}, u32[]{:S(2)}) collective-permute-start(f32[16,48,128]{2,1,0:T(8,128)S(1)} %all_to_all.34.own_ref), channel_id=1, source_target_pairs={{0,1},{1,0},{2,3},{3,2},{4,5},{5,4},{6,7},{7,6},{8,9},{9,8},{10,11... | collective-permute-start | bytes 1179656 | tf_op jit(solution)/shard_map/cond/branch_1_fun/ppermute | solution.py:490
  84.4 0.6 copy-start.3
